TPU v7x, 512 devices: a whole 4x8x8 slice. The times are simulated.
512 devices in a mesh: dx: 4 (over x), dy: 16 (over z, core), solid: 8 (over y).
Axes of the slice: x: 4, y: 8, z: 8, core: 2. Of those that a mesh axis runs over, the one named last changes fastest.
Arguments:
- velocity: float32 [3, 4, 4, 4, 4, 64, 1024], P(None, None, None, None, 'dx', 'dy', 'solid'), may hold values from -6 to 6
- viscosity: float32 [4, 64, 1024], P('dx', 'dy', 'solid'), may hold values from 0.5 to 4
- cell_config: int32 [4, 64, 1024], P('dx', 'dy', 'solid'), may hold values from 0 to 7
- constraint_offsets: float32 [8, 64, 64], replicated, may hold values from -0.24 to 0.24
- slot_cells: int32 [4, 128, 1024], P('dx', ('dy', 'solid')), may hold values from -1 to 511, as said below
- point_coords: float32 [3, 4, 128, 1024], P(None, 'dx', ('dy', 'solid')), may hold values from 0 to 1
- strain_offsets: float32 [3, 3, 4, 128, 1024], P(None, None, 'dx', ('dy', 'solid')), may hold values from -1.5 to 1.5
- solid_velocity: float32 [3, 4, 128, 1024], P(None, 'dx', ('dy', 'solid')), may hold values from -6 to 6
Outputs:
- fluid_out: float32 [3, 4, 4, 4, 4, 64, 1024], P(None, None, None, None, 'dx', 'dy', 'solid')
- new_deform: float32 [3, 3, 4, 128, 1024], P(None, None, 'dx', ('dy', 'solid'))
Inputs may be any that keep to these rules, and one draw needn't show every extreme that they name: `slot_cells`: an entry is -1 for an empty slot, else a cell of the owner numbered with x slowest and z fastest. Slots h * 8 to (h + 1) * 8 - 1 of owner o hold the points that device h keeps.
All inputs are finite; a program needn't handle non-finite values.
Results may differ from a plain program's by a relative error of at most 0.0003.
Values sent between devices are 32-bit elements; how exact they have to be, the bound alone decides.
A program may use at most 64 MiB of HBM per device.

v0:
```python
import jax
import jax.numpy as jnp
import numpy as np
from jax import lax
from jax.sharding import PartitionSpec as P

NCONF = 8


PRECISE = lax.Precision.HIGHEST
TIME_STEP = 0.05
SPRING_RATE = 2.0
PENALTY = 4.0
STIFFNESS = np.array(
    [[2.0, -1.0, 0.0, 0.0], [-1.0, 2.0, -1.0, 0.0], [0.0, -1.0, 2.0, -1.0], [0.0, 0.0, -1.0, 2.0]]
)
NODE_POINTS = (0.0, 1.0 / 3.0, 2.0 / 3.0, 1.0)


def extended(shard, sides, width):
    for axis, dim in sides:
        peers, length = (lax.axis_size(axis), shard.shape[dim])
        up = [(i, (i + 1) % peers) for i in range(peers - 1)]
        down = [(j, i) for i, j in up]
        last = lax.slice_in_dim(shard, length - width, length, axis=dim)
        initial = lax.slice_in_dim(shard, 0, width, axis=dim)
        before = lax.ppermute(last, axis, up)
        after = lax.ppermute(initial, axis, down)
        shard = jnp.concatenate([before, shard, after], axis=dim)
    return shard


def lagrange(coord):
    values = []
    slopes = []
    for which in range(4):
        others = [NODE_POINTS[j] for j in range(4) if j != which]
        denom = 1.0
        for other in others:
            denom = denom * (NODE_POINTS[which] - other)
        first = coord - others[0]
        second = coord - others[1]
        third = coord - others[2]
        values.append(first * second * third / denom)
        slopes.append((second * third + first * third + first * second) / denom)
    return (jnp.stack(values), jnp.stack(slopes))


def constrain(flat, config, offsets, transpose):
    eye = jnp.eye(64, dtype=flat.dtype)
    result = jnp.zeros_like(flat)
    for which in range(NCONF):
        matrix = eye + offsets[which]
        form = "ji,mjn->min" if transpose else "ij,mjn->min"
        product = jnp.einsum(form, matrix, flat, precision=PRECISE)
        result = result + jnp.where(config == which, product, 0.0)
    return result


def operate(field, planes, viscosity):
    lower_x, upper_x, lower_y, upper_y, lower_z, upper_z = planes
    stiff = jnp.asarray(STIFFNESS, field.dtype)
    lap = jnp.einsum("ia,kabcxyz->kibcxyz", stiff, field, precision=PRECISE)
    lap = lap + jnp.einsum("ib,kabcxyz->kaicxyz", stiff, field, precision=PRECISE)
    lap = lap + jnp.einsum("ic,kabcxyz->kabixyz", stiff, field, precision=PRECISE)
    result = field + viscosity * lap
    result = result.at[:, 0].add(PENALTY * (field[:, 0] - lower_x))
    result = result.at[:, 3].add(PENALTY * (field[:, 3] - upper_x))
    result = result.at[:, :, 0].add(PENALTY * (field[:, :, 0] - lower_y))
    result = result.at[:, :, 3].add(PENALTY * (field[:, :, 3] - upper_y))
    result = result.at[:, :, :, 0].add(PENALTY * (field[:, :, :, 0] - lower_z))
    result = result.at[:, :, :, 3].add(PENALTY * (field[:, :, :, 3] - upper_z))
    return result


def evaluate(gathered, coords):
    field = gathered.reshape(3, 4, 4, 4, -1)
    value_x, slope_x = lagrange(coords[0])
    value_y, slope_y = lagrange(coords[1])
    value_z, slope_z = lagrange(coords[2])
    along_zp = jnp.einsum("kabcs,cs->kabs", field, value_z, precision=PRECISE)
    along_zd = jnp.einsum("kabcs,cs->kabs", field, slope_z, precision=PRECISE)
    plain = jnp.einsum("kabs,bs->kas", along_zp, value_y, precision=PRECISE)
    dery = jnp.einsum("kabs,bs->kas", along_zp, slope_y, precision=PRECISE)
    derz = jnp.einsum("kabs,bs->kas", along_zd, value_y, precision=PRECISE)
    vel = jnp.einsum("kas,as->ks", plain, value_x, precision=PRECISE)
    grad_x = jnp.einsum("kas,as->ks", plain, slope_x, precision=PRECISE)
    grad_y = jnp.einsum("kas,as->ks", dery, value_x, precision=PRECISE)
    grad_z = jnp.einsum("kas,as->ks", derz, value_x, precision=PRECISE)
    return (vel, jnp.stack([grad_x, grad_y, grad_z], axis=1))


def solid_update(vel, grad, strain, motion):
    eye = jnp.eye(3, dtype=strain.dtype)[:, :, None]
    deform = eye + strain
    moved = deform + TIME_STEP * jnp.einsum("kjs,jls->kls", grad, deform, precision=PRECISE)
    stress = jnp.einsum("kls,mls->kms", moved, moved, precision=PRECISE) - eye
    drag = SPRING_RATE * (motion - vel)
    return (moved, stress, drag)


def spread_nodes(stress, drag, coords):
    value_x, slope_x = lagrange(coords[0])
    value_y, slope_y = lagrange(coords[1])
    value_z, slope_z = lagrange(coords[2])
    shape_x = jnp.einsum("as,bs,cs->abcs", slope_x, value_y, value_z, precision=PRECISE)
    shape_y = jnp.einsum("as,bs,cs->abcs", value_x, slope_y, value_z, precision=PRECISE)
    shape_z = jnp.einsum("as,bs,cs->abcs", value_x, value_y, slope_z, precision=PRECISE)
    whole = jnp.einsum("as,bs,cs->abcs", value_x, value_y, value_z, precision=PRECISE)
    nodal = jnp.einsum("ks,abcs->kabcs", stress[:, 0], shape_x, precision=PRECISE)
    nodal = nodal + jnp.einsum("ks,abcs->kabcs", stress[:, 1], shape_y, precision=PRECISE)
    nodal = nodal + jnp.einsum("ks,abcs->kabcs", stress[:, 2], shape_z, precision=PRECISE)
    nodal = jnp.einsum("ks,abcs->kabcs", drag, whole, precision=PRECISE) - nodal
    return nodal.reshape(192, -1)


def shards(
    velocity,
    viscosity,
    cell_config,
    constraint_offsets,
    slot_cells,
    point_coords,
    strain_offsets,
    solid_velocity,
):
    shape = velocity.shape
    count = shape[4] * shape[5] * shape[6]
    config = cell_config.reshape(count)
    flat = constrain(velocity.reshape(3, 64, count), config, constraint_offsets, False)
    constrained = flat.reshape(shape)
    padded = extended(constrained, (("dx", 4), ("dy", 5), ("solid", 6)), 1)
    planes = (
        padded[:, 3, :, :, :-2, 1:-1, 1:-1],
        padded[:, 0, :, :, 2:, 1:-1, 1:-1],
        padded[:, :, 3, :, 1:-1, :-2, 1:-1],
        padded[:, :, 0, :, 1:-1, 2:, 1:-1],
        padded[:, :, :, 3, 1:-1, 1:-1, :-2],
        padded[:, :, :, 0, 1:-1, 1:-1, 2:],
    )
    applied = operate(constrained, planes, viscosity)
    block = flat.reshape(192, count)
    targets = slot_cells[0, 0]
    live = targets >= 0
    safe = jnp.where(live, targets, 0)
    coords = point_coords[:, 0, 0]
    strain = strain_offsets[:, :, 0, 0]
    motion = solid_velocity[:, 0, 0]
    gathered = jnp.where(live[None, :], jnp.take(block, safe, axis=1), 0.0)
    vel, grad = evaluate(gathered, coords)
    packed = jnp.concatenate([vel, grad.reshape(9, -1)], axis=0)
    received = lax.all_to_all(packed, ("dy", "solid"), split_axis=1, concat_axis=1, tiled=True)
    moved, stress, drag = solid_update(received[:3], received[3:].reshape(3, 3, -1), strain, motion)
    reply = jnp.concatenate([stress.reshape(9, -1), drag], axis=0)
    returned = lax.all_to_all(reply, ("dy", "solid"), split_axis=1, concat_axis=1, tiled=True)
    nodal = spread_nodes(returned[:9].reshape(3, 3, -1), returned[9:], coords)
    nodal = jnp.where(live[None, :], nodal, 0.0)
    force = jnp.zeros_like(block).at[:, safe].add(nodal)
    total = applied.reshape(3, 64, count) - force.reshape(3, 64, count)
    fluid_out = constrain(total, config, constraint_offsets, True).reshape(shape)
    return (fluid_out, moved[:, :, None, None, :])


def solution(mesh):
    return jax.shard_map(
        shards,
        mesh=mesh,
        in_specs=(
            P(None, None, None, None, "dx", "dy", "solid"),
            P("dx", "dy", "solid"),
            P("dx", "dy", "solid"),
            P(),
            P("dx", ("dy", "solid"), None),
            P(None, "dx", ("dy", "solid"), None),
            P(None, None, "dx", ("dy", "solid"), None),
            P(None, "dx", ("dy", "solid"), None),
        ),
        out_specs=(
            P(None, None, None, None, "dx", "dy", "solid"),
            P(None, None, "dx", ("dy", "solid"), None),
        ),
        check_vma=False,
    )
```

profile of v0, /device:TPU:1, one launch (start us, length us, event | category | flops | bytes accessed | tf_op | source)
XLA Modules:
  0.0 200.1 jit_solution(8097012964828898201)
XLA Ops:
  0.6 1.2 reshape.1161
  1.8 0.7 compare_bitcast_fusion.7
  2.6 1.2 convolution_select_fusion.8
  3.8 1.2 convolution_select_fusion.9
  7.6 0.6 fusion.7
  8.3 1.0 copy.359
  9.3 4.7 %collective-permute-start = (f32[3,4,4,4,1,4,128]{6,1,5,3,2,0,4:T(4,128)}, f32[3,4,4,4,1,4,128]{6,1,5,3,2,0,4:T(4,128)}, u32[]{:S(2)}, u32[]{:S(2)}) collective-permute-start(f32[3,4,4,4,1,4,128]{6,1,5,3,2,0,4:T(4,128)} %copy.359), channel_id=1, source_target_pairs={{0,128},{128,256},{256,384},{1,129},{129,257},{257,385},{2,130},{1... | collective-permute-start | bytes 1179656 | tf_op jit(solution)/shard_map/ppermute | solution.py:27
  14.0 1.3 collective-permute-start.1
  15.7 3.5 %gather_fusion = f32[1024,192]{1,0:T(8,128)S(1)} fusion(f32[192,512]{0,1:T(8,128)S(1)} %copy.374, s32[1024]{0:T(1024)S(1)} %broadcast_clamp_fusion), kind=kCustom, calls=%fused_computation | custom fusion | bytes 1576960 | tf_op jit(solution)/shard_map/jit(_take)/gather | solution.py:149
  19.8 1.1 multiply_reduce_fusion.1
  22.2 1.6 copy.377
  23.8 29.6 %all-to-all-start = ((f32[12,128,8]{0,2,1:T(8,128)}), f32[12,128,8]{0,2,1:T(8,128)S(1)}, u32[]{:S(2)}, u32[]{:S(2)}) async-start(f32[12,128,8]{0,2,1:T(8,128)} %copy.377), calls=%async_computation | async-start | bytes 1048576 | tf_op jit(solution)/shard_map/all_to_all | solution.py:152
  53.6 0.8 fusion.21
  54.4 0.8 fusion.23
  55.3 0.7 broadcast_multiply_fusion.1
  56.2 1.8 copy.373
  57.9 1.6 fusion.19
  59.5 13.2 %all-to-all-done = f32[12,128,8]{0,2,1:T(8,128)S(1)} async-done(((f32[12,128,8]{0,2,1:T(8,128)}), f32[12,128,8]{0,2,1:T(8,128)S(1)}, u32[]{:S(2)}, u32[]{:S(2)}) %all-to-all-start) | async-done | bytes 49184 | tf_op jit(solution)/shard_map/all_to_all | solution.py:152
  72.7 0.9 copy.478
  73.8 1.8 reshape.1221
  75.6 9.9 %bitcast_add_fusion = f32[3,3,1024]{0,1,2:T(4,128)S(1)} fusion(f32[3,3,1,1,1024]{0,1,4,3,2:T(4,128)} %copy.373, f32[3,3,1024]{1,0,2:T(4,128)} %reshape.1221, f32[3,3]{0,1:T(4,128)S(1)} %fusion.88), kind=kOutput, calls=%fused_computation.3 | convolution fusion | flops 368640 | bytes 110628 | tf_op jit(solution)/shard_map/kjs,jls->kls/dot_general | solution.py:96
  85.5 9.5 %bitcast_subtract_fusion = f32[3,3,1024]{0,1,2:T(4,128)} fusion(f32[3,3,1024]{0,1,2:T(4,128)S(1)} %bitcast_add_fusion, f32[3,3]{0,1:T(4,128)S(1)} %fusion.88), kind=kOutput, calls=%fused_computation.2 | convolution fusion | flops 340992 | bytes 73764 | tf_op jit(solution)/shard_map/kls,mls->kms/dot_general | solution.py:97
  95.0 2.3 %copy.382 = f32[3,3,1024]{2,1,0:T(4,128)S(1)} copy(f32[3,3,1024]{0,1,2:T(4,128)} %bitcast_subtract_fusion) | data formatting | bytes 73728 | tf_op jit(solution)/shard_map/sub | solution.py:97
  97.3 1.2 concatenate.54
  98.5 2.1 %pad_maximum_fusion.2 = f32[12,128,8]{2,1,0:T(8,128)} fusion(f32[3,128,8]{2,1,0:T(8,128)S(1)} %subtract_multiply_fusion, f32[9,128,8]{2,1,0:T(8,128)} %concatenate.54), kind=kLoop, calls=%fused_computation.45 | loop fusion | flops 12288 | bytes 98304 | tf_op jit(solution)/shard_map/concatenate | solution.py:154
  100.6 2.8 %copy.384 = f32[12,128,8]{0,2,1:T(8,128)} copy(f32[12,128,8]{2,1,0:T(8,128)} %pad_maximum_fusion.2) | data formatting | bytes 98304 | tf_op jit(solution)/shard_map/concatenate | solution.py:154
  103.4 7.2 %all-to-all-start.1 = ((f32[12,128,8]{0,2,1:T(8,128)}), f32[12,128,8]{0,2,1:T(8,128)}, u32[]{:S(2)}, u32[]{:S(2)}) async-start(f32[12,128,8]{0,2,1:T(8,128)} %copy.384), calls=%async_computation.1 | async-start | bytes 1048576 | tf_op jit(solution)/shard_map/all_to_all | solution.py:155
  110.6 1.1 multiply_bitcast_fusion.3
  111.7 1.3 copy.400
  113.0 16.6 %all-to-all-done.1 = f32[12,128,8]{0,2,1:T(8,128)} async-done(((f32[12,128,8]{0,2,1:T(8,128)}), f32[12,128,8]{0,2,1:T(8,128)}, u32[]{:S(2)}, u32[]{:S(2)}) %all-to-all-start.1) | async-done | bytes 49184 | tf_op jit(solution)/shard_map/all_to_all | solution.py:155
  129.6 1.9 copy.386
  131.9 1.2 slice_bitcast_fusion
  134.5 6.3 %scatter_custom_fusion = f32[192,512]{0,1:T(8,128)S(1)} fusion(s32[1024]{0:T(1024)} %bitcast.470, f32[1024,192]{1,0:T(8,128)S(1)} %copy.387, f32[]{:T(128)} %constant.226.clone.1), kind=kCustom, calls=%fused_computation.62 | custom fusion | flops 196608 | bytes 393728 | tf_op jit(solution)/shard_map/scatter-add | solution.py:158
  141.0 0.9 reshape.1168
  141.9 1.0 constant_dynamic-update-slice_fusion.2
  143.2 1.0 constant_dynamic-update-slice_fusion
  144.4 3.0 %collective-permute-start.2 = (f32[3,4,4,4,3,1,128]{6,1,5,3,2,0,4:T(4,128)S(1)}, f32[3,4,4,4,3,1,128]{6,1,5,3,2,0,4:T(4,128)S(1)}, u32[]{:S(2)}, u32[]{:S(2)}) collective-permute-start(f32[3,4,4,4,3,1,128]{6,1,5,3,2,0,4:T(4,128)S(1)} %get-tuple-element.104), channel_id=1, source_target_pairs={{0,8},{8,16},{16,24},{24,32},{32,40},{40,48},{48,56},{56,64},{64,7... | collective-permute-start | bytes 884744 | tf_op jit(solution)/shard_map/ppermute | solution.py:27
  147.4 1.9 collective-permute-start.3
  149.3 1.3 fusion.50
  150.6 2.2 %scatter-add.26 = f32[3,4,4,4,1,4,128]{6,1,5,3,2,0,4:T(4,128)S(1)} dynamic-update-slice(f32[3,4,4,4,1,4,128]{6,1,5,3,2,0,4:T(4,128)S(1)} %fusion.19, f32[3,1,4,4,1,4,128]{6,1,5,3,2,0,4:T(1,128)S(1)} %fusion.50, s32[]{:T(128)} %constant.225.clone.1, s32[]{:T(128)} %constant.225.clone.1, s32[]{:T(128)} %constant.225.clone.1, s32[]{:T(128)} %constant.225.clone.1, s32[]{:T(128)} %constant.225.clone.1, ...) | dynamic-update-slice | bytes 196612 | tf_op jit(solution)/shard_map/scatter-add | solution.py:67
  152.8 1.4 fusion.48
  154.2 2.0 %scatter-add.29 = f32[3,4,4,4,1,4,128]{6,1,5,3,2,0,4:T(4,128)S(1)} dynamic-update-slice(f32[3,4,4,4,1,4,128]{6,1,5,3,2,0,4:T(4,128)S(1)} %scatter-add.26, f32[3,1,4,4,1,4,128]{6,1,5,3,2,0,4:T(1,128)S(1)} %fusion.48, s32[]{:T(128)} %constant.225.clone.1, s32[]{:T(128)} %constant.229.clone.1, s32[]{:T(128)} %constant.225.clone.1, s32[]{:T(128)} %constant.225.clone.1, s32[]{:T(128)} %constant.225.clone.1, ...) | dynamic-update-slice | bytes 196612 | tf_op jit(solution)/shard_map/scatter-add | solution.py:68
  156.2 0.7 copy-done.1
  156.9 0.7 copy-done.3
  158.1 2.6 %fusion.89 = (f32[3,4,4,4,3,6,1]{6,1,5,3,2,0,4:T(4,128)S(1)}, f32[3,4,4,4,3,6,1]{6,1,5,3,2,0,4:T(4,128)}) fusion(f32[3,4,4,4,3,6,128]{6,1,5,3,2,0,4:T(4,128)S(1)} %pad_maximum_fusion), kind=kLoop, calls=%fused_computation.209 | loop fusion | bytes 55296 | tf_op jit(solution)/shard_map/slice | solution.py:26
  160.7 5.4 %copy.368 = f32[3,4,4,4,3,6,1]{5,3,6,4,2,1,0:T(4,128)} copy(f32[3,4,4,4,3,6,1]{6,1,5,3,2,0,4:T(4,128)} %get-tuple-element.102) | data formatting | bytes 27648 | tf_op jit(solution)/shard_map/slice | solution.py:25
  166.0 3.5 %collective-permute-start.4 = (f32[3,4,4,4,3,6,1]{5,3,6,4,2,1,0:T(4,128)}, f32[3,4,4,4,3,6,1]{5,3,6,4,2,1,0:T(4,128)}, u32[]{:S(2)}, u32[]{:S(2)}) collective-permute-start(f32[3,4,4,4,3,6,1]{5,3,6,4,2,1,0:T(4,128)} %copy.368), channel_id=1, source_target_pairs={{0,1},{1,2},{2,3},{3,4},{4,5},{5,6},{6,7},{8,9},{9,10},{10,11},{11... | collective-permute-start | bytes 41480 | tf_op jit(solution)/shard_map/ppermute | solution.py:27
  169.6 4.4 %copy.371 = f32[3,4,4,4,3,6,1]{5,3,6,4,2,1,0:T(4,128)} copy(f32[3,4,4,4,3,6,1]{6,1,5,3,2,0,4:T(4,128)S(1)} %get-tuple-element.101) | data formatting | bytes 27648 | tf_op jit(solution)/shard_map/slice | solution.py:26
  174.0 1.4 collective-permute-start.5
  175.4 1.0 fusion.46
  176.4 1.0 fusion.42
  177.4 4.7 %copy.369 = f32[3,4,4,4,3,6,1]{6,1,5,3,2,0,4:T(4,128)S(1)} copy(f32[3,4,4,4,3,6,1]{5,3,6,4,2,1,0:T(4,128)} %collective-permute-done.4) | data formatting | bytes 27648 | tf_op jit(solution)/shard_map/ppermute | solution.py:27
  182.1 2.9 %collective-permute-done.5 = f32[3,4,4,4,3,6,1]{5,3,6,4,2,1,0:T(4,128)} collective-permute-done((f32[3,4,4,4,3,6,1]{5,3,6,4,2,1,0:T(4,128)}, f32[3,4,4,4,3,6,1]{5,3,6,4,2,1,0:T(4,128)}, u32[]{:S(2)}, u32[]{:S(2)}) %collective-permute-start.5) | collective-permute-done | bytes 13856 | tf_op jit(solution)/shard_map/ppermute | solution.py:28
  185.0 5.6 %copy.372 = f32[3,4,4,4,3,6,1]{6,1,5,3,2,0,4:T(4,128)} copy(f32[3,4,4,4,3,6,1]{5,3,6,4,2,1,0:T(4,128)} %collective-permute-done.5) | data formatting | bytes 27648 | tf_op jit(solution)/shard_map/ppermute | solution.py:28
  190.6 1.3 fusion.38
  192.2 1.3 fusion.34
  195.0 0.5 convolution_select_fusion.1
  195.6 0.5 convolution_select_fusion.2
  196.1 0.5 convolution_select_fusion.3
  196.7 0.5 convolution_select_fusion.4
  197.2 0.5 convolution_select_fusion.5
  197.7 0.5 convolution_select_fusion.6
  198.3 0.7 fusion.15
  199.0 0.9 reshape.1169
  (133 shorter events, 9.8 us)
Async XLA Ops:
  0.6 4.4 %copy-start.7 = (f32[8,64,64]{2,1,0:T(8,128)S(1)}, f32[8,64,64]{2,1,0:T(8,128)}, u32[]{:S(2)}) copy-start(f32[8,64,64]{2,1,0:T(8,128)} %param.24) | copy-start | bytes 393220
  2.5 4.0 %copy-start.28 = (pred[512]{0:T(512)(128)(4,1)}, pred[512]{0:T(512)(128)(4,1)S(1)}, u32[]{:S(2)}) copy-start(pred[512]{0:T(512)(128)(4,1)S(1)} %get-tuple-element.144) | copy-start | bytes 1540
  2.5 4.0 %copy-start.30 = (pred[512]{0:T(512)(128)(4,1)}, pred[512]{0:T(512)(128)(4,1)S(1)}, u32[]{:S(2)}) copy-start(pred[512]{0:T(512)(128)(4,1)S(1)} %get-tuple-element.143) | copy-start | bytes 1540
  2.5 4.0 %copy-start.32 = (pred[512]{0:T(512)(128)(4,1)}, pred[512]{0:T(512)(128)(4,1)S(1)}, u32[]{:S(2)}) copy-start(pred[512]{0:T(512)(128)(4,1)S(1)} %get-tuple-element.142) | copy-start | bytes 1540
  2.6 4.0 %copy-start.34 = (pred[512]{0:T(512)(128)(4,1)}, pred[512]{0:T(512)(128)(4,1)S(1)}, u32[]{:S(2)}) copy-start(pred[512]{0:T(512)(128)(4,1)S(1)} %get-tuple-element.148) | copy-start | bytes 1540
  2.6 4.0 %copy-start.36 = (pred[512]{0:T(512)(128)(4,1)}, pred[512]{0:T(512)(128)(4,1)S(1)}, u32[]{:S(2)}) copy-start(pred[512]{0:T(512)(128)(4,1)S(1)} %get-tuple-element.147) | copy-start | bytes 1540
  2.6 4.0 %copy-start.26 = (pred[512]{0:T(512)(128)(4,1)}, pred[512]{0:T(512)(128)(4,1)S(1)}, u32[]{:S(2)}) copy-start(pred[512]{0:T(512)(128)(4,1)S(1)} %get-tuple-element.145) | copy-start | bytes 1540
  2.6 4.5 %copy-start.24 = (pred[512]{0:T(512)(128)(4,1)}, pred[512]{0:T(512)(128)(4,1)S(1)}, u32[]{:S(2)}) copy-start(pred[512]{0:T(512)(128)(4,1)S(1)} %get-tuple-element.146) | copy-start | bytes 1540
  2.6 5.0 %copy-start.38 = (pred[512]{0:T(512)(128)(4,1)}, pred[512]{0:T(512)(128)(4,1)S(1)}, u32[]{:S(2)}) copy-start(pred[512]{0:T(512)(128)(4,1)S(1)} %get-tuple-element.141) | copy-start | bytes 1540
  7.6 7.7 %copy-start.16 = (f32[3,1,1,1024]{3,2,1,0:T(1,128)S(1)}, f32[3,1,1,1024]{3,2,1,0:T(1,128)}, u32[]{:S(2)}) copy-start(f32[3,1,1,1024]{3,2,1,0:T(1,128)} %param.26) | copy-start | bytes 36868
  7.6 7.9 %copy-start.19 = (s32[1,1,1024]{2,1,0:T(1,128)S(1)}, s32[1,1,1024]{2,1,0:T(1,128)}, u32[]{:S(2)}) copy-start(s32[1,1,1024]{2,1,0:T(1,128)} %param.25) | copy-start | bytes 12292
  9.3 132.6 %collective-permute-start = (f32[3,4,4,4,1,4,128]{6,1,5,3,2,0,4:T(4,128)}, f32[3,4,4,4,1,4,128]{6,1,5,3,2,0,4:T(4,128)}, u32[]{:S(2)}, u32[]{:S(2)}) collective-permute-start(f32[3,4,4,4,1,4,128]{6,1,5,3,2,0,4:T(4,128)} %copy.359), channel_id=1, source_target_pairs={{0,128},{128,256},{256,384},{1,129},{129,257},{257,385},{2,130},{1... | collective-permute-start | bytes 1179656 | tf_op jit(solution)/shard_map/ppermute | solution.py:27
  14.0 129.2 %collective-permute-start.1 = (f32[3,4,4,4,1,4,128]{6,1,5,3,2,0,4:T(4,128)}, f32[3,4,4,4,1,4,128]{6,1,5,3,2,0,4:T(4,128)}, u32[]{:S(2)}, u32[]{:S(2)}) collective-permute-start(f32[3,4,4,4,1,4,128]{6,1,5,3,2,0,4:T(4,128)} %copy.359), channel_id=1, source_target_pairs={{128,0},{256,128},{384,256},{129,1},{257,129},{385,257},{130,2},{2... | collective-permute-start | bytes 1179656 | tf_op jit(solution)/shard_map/ppermute | solution.py:28
  15.4 3.7 %copy-start.20 = (s32[1024,1]{0,1:T(1,128)}, s32[1024,1]{0,1:T(1,128)S(1)}, u32[]{:S(2)}) copy-start(s32[1024,1]{0,1:T(1,128)S(1)} %compare_select_fusion) | copy-start | bytes 12292
  19.7 1.3 copy-start.22
  19.8 1.8 copy-start.14
  22.2 31.4 %copy-start.18 = (f32[4,4,1,1,1,1]{1,0,5,4,3,2:T(4,128)S(1)}, f32[4,4,1,1,1,1]{1,0,5,4,3,2:T(4,128)}, u32[]{:S(2)}) copy-start(f32[4,4,1,1,1,1]{1,0,5,4,3,2:T(4,128)} %constant.264) | copy-start | bytes 196
  23.8 32.1 %copy-start.21 = (f32[3,1,1,1024]{3,2,1,0:T(1,128)S(1)}, f32[3,1,1,1024]{3,2,1,0:T(1,128)}, u32[]{:S(2)}) copy-start(f32[3,1,1,1024]{3,2,1,0:T(1,128)} %param.28) | copy-start | bytes 36868
  23.8 32.3 %copy-start.17 = (f32[3,3,1,1,1024]{4,3,2,1,0:T(1,128)S(1)}, f32[3,3,1,1,1024]{4,3,2,1,0:T(1,128)}, u32[]{:S(2)}) copy-start(f32[3,3,1,1,1024]{4,3,2,1,0:T(1,128)} %param.27) | copy-start | bytes 110596
  23.8 48.9 %all-to-all-start = ((f32[12,128,8]{0,2,1:T(8,128)}), f32[12,128,8]{0,2,1:T(8,128)S(1)}, u32[]{:S(2)}, u32[]{:S(2)}) async-start(f32[12,128,8]{0,2,1:T(8,128)} %copy.377), calls=%async_computation | async-start | bytes 1048576 | tf_op jit(solution)/shard_map/all_to_all | solution.py:152
  54.4 3.5 %copy-start.40 = (f32[1,4,128]{2,1,0:T(4,128)S(1)}, f32[1,4,128]{2,1,0:T(4,128)}, u32[]{:S(2)}) copy-start(f32[1,4,128]{2,1,0:T(4,128)} %param.22) | copy-start | bytes 6148
  98.5 12.1 %copy-start.12 = (f32[1024,4,4]{0,1,2:T(4,128)S(1)}, f32[1024,4,4]{0,1,2:T(4,128)}, u32[]{:S(2)}) copy-start(f32[1024,4,4]{0,1,2:T(4,128)} %get-tuple-element.113) | copy-start | bytes 196612
  98.5 12.1 %copy-start.13 = (f32[1024,4,4]{0,1,2:T(4,128)S(1)}, f32[1024,4,4]{0,1,2:T(4,128)}, u32[]{:S(2)}) copy-start(f32[1024,4,4]{0,1,2:T(4,128)} %get-tuple-element.114) | copy-start | bytes 196612
  98.5 12.1 %copy-start.15 = (f32[1024,4]{0,1:T(4,128)S(1)}, f32[1024,4]{0,1:T(4,128)}, u32[]{:S(2)}) copy-start(f32[1024,4]{0,1:T(4,128)} %copy-done.14) | copy-start | bytes 49156
  103.4 26.2 %all-to-all-start.1 = ((f32[12,128,8]{0,2,1:T(8,128)}), f32[12,128,8]{0,2,1:T(8,128)}, u32[]{:S(2)}, u32[]{:S(2)}) async-start(f32[12,128,8]{0,2,1:T(8,128)} %copy.384), calls=%async_computation.1 | async-start | bytes 1048576 | tf_op jit(solution)/shard_map/all_to_all | solution.py:155
  113.0 20.4 %copy-start.9 = (f32[1024,4,4,4]{0,3,2,1:T(4,128)S(1)}, f32[1024,4,4,4]{0,3,2,1:T(4,128)}, u32[]{:S(2)}) copy-start(f32[1024,4,4,4]{0,3,2,1:T(4,128)} %get-tuple-element.106) | copy-start | bytes 786436
  113.0 20.4 %copy-start.10 = (f32[1024,4,4,4]{0,3,2,1:T(4,128)S(1)}, f32[1024,4,4,4]{0,3,2,1:T(4,128)}, u32[]{:S(2)}) copy-start(f32[1024,4,4,4]{0,3,2,1:T(4,128)} %get-tuple-element.110) | copy-start | bytes 786436
  113.0 20.4 %copy-start.11 = (f32[1024,4,4,4]{0,3,2,1:T(4,128)S(1)}, f32[1024,4,4,4]{0,3,2,1:T(4,128)}, u32[]{:S(2)}) copy-start(f32[1024,4,4,4]{0,3,2,1:T(4,128)} %get-tuple-element.111) | copy-start | bytes 786436
  133.4 0.7 copy-start.23
  144.4 11.8 %collective-permute-start.2 = (f32[3,4,4,4,3,1,128]{6,1,5,3,2,0,4:T(4,128)S(1)}, f32[3,4,4,4,3,1,128]{6,1,5,3,2,0,4:T(4,128)S(1)}, u32[]{:S(2)}, u32[]{:S(2)}) collective-permute-start(f32[3,4,4,4,3,1,128]{6,1,5,3,2,0,4:T(4,128)S(1)} %get-tuple-element.104), channel_id=1, source_target_pairs={{0,8},{8,16},{16,24},{24,32},{32,40},{40,48},{48,56},{56,64},{64,7... | collective-permute-start | bytes 884744 | tf_op jit(solution)/shard_map/ppermute | solution.py:27
  147.4 8.8 %collective-permute-start.3 = (f32[3,4,4,4,3,1,128]{6,1,5,3,2,0,4:T(4,128)S(1)}, f32[3,4,4,4,3,1,128]{6,1,5,3,2,0,4:T(4,128)S(1)}, u32[]{:S(2)}, u32[]{:S(2)}) collective-permute-start(f32[3,4,4,4,3,1,128]{6,1,5,3,2,0,4:T(4,128)S(1)} %get-tuple-element.103), channel_id=1, source_target_pairs={{8,0},{16,8},{24,16},{32,24},{40,32},{48,40},{56,48},{64,56},{72,6... | collective-permute-start | bytes 884744 | tf_op jit(solution)/shard_map/ppermute | solution.py:28
  156.2 0.7 copy-start.1
  156.9 0.7 copy-start.3
  166.0 11.3 %collective-permute-start.4 = (f32[3,4,4,4,3,6,1]{5,3,6,4,2,1,0:T(4,128)}, f32[3,4,4,4,3,6,1]{5,3,6,4,2,1,0:T(4,128)}, u32[]{:S(2)}, u32[]{:S(2)}) collective-permute-start(f32[3,4,4,4,3,6,1]{5,3,6,4,2,1,0:T(4,128)} %copy.368), channel_id=1, source_target_pairs={{0,1},{1,2},{2,3},{3,4},{4,5},{5,6},{6,7},{8,9},{9,10},{10,11},{11... | collective-permute-start | bytes 41480 | tf_op jit(solution)/shard_map/ppermute | solution.py:27
  174.0 2.4 %copy-start.4 = (f32[3,4,4,4,3,1,128]{6,1,5,3,2,0,4:T(4,128)S(1)}, f32[3,4,4,4,3,1,128]{6,1,5,3,2,0,4:T(4,128)}, u32[]{:S(2)}) copy-start(f32[3,4,4,4,3,1,128]{6,1,5,3,2,0,4:T(4,128)} %copy-done.3) | copy-start | bytes 884740
  174.0 11.0 %collective-permute-start.5 = (f32[3,4,4,4,3,6,1]{5,3,6,4,2,1,0:T(4,128)}, f32[3,4,4,4,3,6,1]{5,3,6,4,2,1,0:T(4,128)}, u32[]{:S(2)}, u32[]{:S(2)}) collective-permute-start(f32[3,4,4,4,3,6,1]{5,3,6,4,2,1,0:T(4,128)} %copy.371), channel_id=1, source_target_pairs={{1,0},{2,1},{3,2},{4,3},{5,4},{6,5},{7,6},{9,8},{10,9},{11,10},{12... | collective-permute-start | bytes 41480 | tf_op jit(solution)/shard_map/ppermute | solution.py:28
  190.6 1.5 copy-start
  190.6 1.5 copy-start.2
  190.6 1.6 copy-start.5
  192.2 1.3 copy-start.6
  193.5 1.0 copy-start.8
  193.5 1.0 copy-start.37
  193.5 1.5 copy-start.35
  193.8 1.7 copy-start.33
  194.0 2.1 %copy-start.31 = (pred[512]{0:T(512)(128)(4,1)S(1)}, pred[512]{0:T(512)(128)(4,1)}, u32[]{:S(2)}) copy-start(pred[512]{0:T(512)(128)(4,1)} %copy-done.30) | copy-start | bytes 1540
  194.5 2.2 %copy-start.29 = (pred[512]{0:T(512)(128)(4,1)S(1)}, pred[512]{0:T(512)(128)(4,1)}, u32[]{:S(2)}) copy-start(pred[512]{0:T(512)(128)(4,1)} %copy-done.28) | copy-start | bytes 1540
  195.0 2.2 %copy-start.27 = (pred[512]{0:T(512)(128)(4,1)S(1)}, pred[512]{0:T(512)(128)(4,1)}, u32[]{:S(2)}) copy-start(pred[512]{0:T(512)(128)(4,1)} %copy-done.26) | copy-start | bytes 1540
  195.6 2.2 %copy-start.25 = (pred[512]{0:T(512)(128)(4,1)S(1)}, pred[512]{0:T(512)(128)(4,1)}, u32[]{:S(2)}) copy-start(pred[512]{0:T(512)(128)(4,1)} %copy-done.24) | copy-start | bytes 1540
  196.1 2.2 %copy-start.39 = (pred[512]{0:T(512)(128)(4,1)S(1)}, pred[512]{0:T(512)(128)(4,1)}, u32[]{:S(2)}) copy-start(pred[512]{0:T(512)(128)(4,1)} %copy-done.38) | copy-start | bytes 1540
where the time goes:
time: 203 us; the launch traced here: 200 us
  local copies, waits for them, and re-layouts  59.2 us (29%)
  starting transfers between devices  52.5 us (26%)
  waiting for transfers between devices  32.7 us (16%)
  matrix products  32.4 us (16%)
  other arithmetic  21.4 us (11%)
    all_to_all x1, starting transfers between devices, shards(): lax.all_to_all(packed, ('dy', 'solid'), split_axis=1, concat_axis=1, tile...  29.6 us
    all_to_all x1, waiting for transfers between devices, shards(): lax.all_to_all(reply, ('dy', 'solid'), split_axis=1, concat_axis=1, tiled...  16.6 us
    all_to_all x1, waiting for transfers between devices, shards(): lax.all_to_all(packed, ('dy', 'solid'), split_axis=1, concat_axis=1, tile...  13.2 us
    ppermute x3, starting transfers between devices, extended(): before = lax.ppermute(last, axis, up)  11.2 us
    dot_general x1, matrix products, solid_update(): jnp.einsum('kjs,jls->kls', grad, deform, precision=PRECISE)  9.88 us
    dot_general x16, matrix products, constrain(): product = jnp.einsum(form, matrix, flat, precision=PRECISE)  9.75 us
    dot_general x1, matrix products, solid_update(): stress = jnp.einsum('kls,mls->kms', moved, moved, precision=PRECISE) - eye  9.51 us
    unnamed x90, local copies, waits for them, and re-layouts  7.53 us
  transfers between devices with their start and end apart: 8, of which 3 were waited for; matrix products, arithmetic and copies ran while one was open for 39% of the time, Pallas kernels for 0%

commit v1 on v0

v1 whole, which is shorter than its diff:
```python
import jax
import jax.numpy as jnp
from jax import lax
from jax.experimental import pallas as pl
from jax.experimental.pallas import tpu as pltpu
from jax.sharding import PartitionSpec as P

F32 = jnp.float32
BF16 = jnp.bfloat16
TIME_STEP = 0.05
SPRING_RATE = 2.0
PENALTY = 4.0
NODE_POINTS = (0.0, 1.0 / 3.0, 2.0 / 3.0, 1.0)
N_DX, N_DY, N_SOLID = 4, 16, 8
MESH = pl.DeviceIdType.MESH


def iota(shape, dim):
    return lax.broadcasted_iota(jnp.int32, shape, dim)


def split(x):
    high = x.astype(BF16)
    return high, (x - high.astype(F32)).astype(BF16)


def dot(a, b):
    return lax.dot_general(a, b, (((1,), (0,)), ((), ())), preferred_element_type=F32)


def dot_nt(a, b):
    return lax.dot_general(a, b, (((1,), (1,)), ((), ())), preferred_element_type=F32)


def lagrange(coord):
    values = []
    slopes = []
    for which in range(4):
        others = [NODE_POINTS[j] for j in range(4) if j != which]
        denom = 1.0
        for other in others:
            denom = denom * (NODE_POINTS[which] - other)
        first = coord - others[0]
        second = coord - others[1]
        third = coord - others[2]
        scale = 1.0 / denom
        values.append(first * second * third * scale)
        slopes.append((second * third + first * third + first * second) * scale)
    return values, slopes


def pick(rows, index):
    out = jnp.where(index == 0, rows[0], rows[1])
    return jnp.where(index < 2, out, jnp.where(index == 2, rows[2], rows[3]))


def stiffness():
    row, col = iota((64, 64), 0), iota((64, 64), 1)
    total = jnp.where(row == col, 6.0, 0.0)
    for step in (16, 4, 1):
        place_row, place_col = (row // step) % 4, (col // step) % 4
        same = (row - place_row * step) == (col - place_col * step)
        near = jnp.abs(place_row - place_col) == 1
        total = total - jnp.where(same & near, 1.0, 0.0)
    return total


def left_operand(stack):
    high, low = split(stack)
    return jnp.concatenate([high, high, low], axis=1)


def constrain(field, left, config):
    high, low = split(field)
    product = dot(left, jnp.concatenate([high, low, high], axis=0))
    total = field
    for which in range(8):
        total = total + jnp.where(config == which, product[which * 64 : which * 64 + 64], 0.0)
    return total


def kernel(
    vel_hbm, visc_hbm, config_hbm, offsets_hbm, cells_hbm, coords_hbm, strain_hbm, motion_hbm,
    fluid_hbm, deform_hbm,
    vel, visc, config, offsets, cells, items,
    field, halves, applied, onehot, shapes, nodal, results, turned,
    packet, middle, arrived, reply, reply_middle, reply_arrived, reply_turned,
    edge, low_x, high_x, low_y, high_y, low_z, high_z,
    fluid, deform,
    in_sem, own_sem, out_sem,
    send_a, recv_a, send_b, recv_b, send_c, recv_c, send_d, recv_d, send_h, recv_h,
):
    me_x, me_y, me_s = lax.axis_index("dx"), lax.axis_index("dy"), lax.axis_index("solid")

    loads = [
        pltpu.make_async_copy(source, target, in_sem.at[which])
        for which, (source, target) in enumerate(
            (
                (strain_hbm, items.at[0:72]),
                (motion_hbm, items.at[72:96]),
                (coords_hbm, items.at[96:120]),
                (cells_hbm, cells),
                (vel_hbm, vel),
                (offsets_hbm, offsets),
                (config_hbm, config),
                (visc_hbm, visc),
            )
        )
    ]
    for load in loads:
        load.start()

    barrier = pltpu.get_barrier_semaphore()
    for step in range(1, N_SOLID):
        pl.semaphore_signal(barrier, inc=1, device_id={"solid": lax.rem(me_s + step, N_SOLID)}, device_id_type=MESH)
    for step in range(1, N_DY):
        pl.semaphore_signal(barrier, inc=1, device_id={"dy": lax.rem(me_y + step, N_DY)}, device_id_type=MESH)
    for step in (1, N_DX - 1):
        pl.semaphore_signal(barrier, inc=1, device_id={"dx": lax.rem(me_x + step, N_DX)}, device_id_type=MESH)

    def over_solid(source, target, send, recv, own):
        copies = [pltpu.make_async_copy(source.at[:, me_s], target.at[:, me_s], own)]
        for step in range(1, N_SOLID):
            peer = lax.rem(me_s + step, N_SOLID)
            copies.append(
                pltpu.make_async_remote_copy(
                    src_ref=source.at[:, peer],
                    dst_ref=target.at[:, me_s],
                    send_sem=send.at[step - 1],
                    recv_sem=recv.at[step - 1],
                    device_id={"solid": peer},
                    device_id_type=MESH,
                )
            )
        return copies

    def over_dy(source, target, send, recv, own):
        copies = [pltpu.make_async_copy(source.at[me_y], target.at[me_y], own)]
        for step in range(1, N_DY):
            peer = lax.rem(me_y + step, N_DY)
            copies.append(
                pltpu.make_async_remote_copy(
                    src_ref=source.at[peer],
                    dst_ref=target.at[me_y],
                    send_sem=send.at[step - 1],
                    recv_sem=recv.at[step - 1],
                    device_id={"dy": peer},
                    device_id_type=MESH,
                )
            )
        return copies

    def start(copies):
        for copy in copies:
            copy.start()

    def arrive(copies):
        copies[0].wait()
        for copy in copies[1:]:
            copy.wait_recv()

    slot_place = iota((1, 1024), 1) & 7
    for load in loads[:4]:
        load.wait()
    items[120:128, :] = cells[...].astype(F32)
    rows = jnp.concatenate([items[pl.ds(g, 16, stride=8), :] for g in range(8)], axis=1)
    spread = jnp.concatenate([jnp.where(slot_place == c, rows, 0.0) for c in range(8)], axis=0)
    spread_high, spread_low = split(spread)
    slot_device = jnp.where((iota((1024, 128), 0) >> 3) == iota((1024, 128), 1), 1.0, 0.0).astype(BF16)
    packed = dot(spread_high, slot_device) + dot(spread_low, slot_device)
    packet[...] = packed.T.reshape(16, 8, 128)
    turned[...] = packed
    reply_turned[...] = jnp.zeros_like(reply_turned)

    pl.semaphore_wait(barrier, N_SOLID - 1 + N_DY - 1 + 2)
    first = over_solid(packet, middle, send_a, recv_a, own_sem.at[0])
    start(first)

    for load in loads[4:]:
        load.wait()
    own_config = config[...]
    config_row = jnp.concatenate([own_config[y : y + 1] for y in range(4)], axis=1)
    left = left_operand(offsets[...].reshape(512, 64))
    for k in range(3):
        start_field = jnp.concatenate([vel[pl.ds(k * 256 + y, 64, stride=4), :] for y in range(4)], axis=1)
        own = constrain(start_field, left, config_row)
        field[k] = own.reshape(4, 16, 512)
        high, low = split(own)
        halves[k * 64 : k * 64 + 64] = high
        halves[192 + k * 64 : 192 + k * 64 + 64] = low

    def remote(source, target, which, where):
        return pltpu.make_async_remote_copy(
            src_ref=source, dst_ref=target, send_sem=send_h.at[which], recv_sem=recv_h.at[which],
            device_id=where, device_id_type=MESH,
        )

    up_x, down_x = lax.rem(me_x + 1, N_DX), lax.rem(me_x + N_DX - 1, N_DX)
    up_y, down_y = lax.rem(me_y + 1, N_DY), lax.rem(me_y + N_DY - 1, N_DY)
    up_s, down_s = lax.rem(me_s + 1, N_SOLID), lax.rem(me_s + N_SOLID - 1, N_SOLID)
    halo = [
        remote(field.at[:, 3], low_x, 0, {"dx": up_x}),
        remote(field.at[:, 0], high_x, 1, {"dx": down_x}),
        remote(field.at[:, :, 8:16, 384:512], low_y, 2, {"dy": up_y}),
        remote(field.at[:, :, 0:8, 0:128], high_y, 3, {"dy": down_y}),
        remote(edge.at[0], low_z, 4, {"solid": up_s}),
        remote(edge.at[1], high_z, 5, {"solid": down_s}),
    ]
    edge_row, edge_col = iota((16, 512), 0), iota((16, 512), 1)
    lane_edge = jnp.where(edge_row < 8, 127, 0)
    edge_pick = jnp.where(
        (edge_col == (edge_row & 7) * 128 + lane_edge) & ((edge_row & 7) < 4), 1.0, 0.0
    ).astype(BF16)
    edges = dot_nt(edge_pick, halves[0:192]) + dot_nt(edge_pick, halves[192:384])
    edge[...] = edges.reshape(2, 8, 192)

    arrive(first)
    second = over_dy(middle, arrived, send_b, recv_b, own_sem.at[1])
    start(second)
    start(halo)

    points = [turned[pl.ds(12 + j, 8, stride=16), :] for j in range(3)]
    target = turned[pl.ds(15, 8, stride=16), :]
    polys = [lagrange(point) for point in points]
    cell_index = iota((512, 256), 0).astype(F32)
    node_row = iota((16, 256), 0)
    for pair in range(4):
        lanes = slice(pair * 256, pair * 256 + 256)

        def row(x):
            return jnp.concatenate([x[2 * pair : 2 * pair + 1], x[2 * pair + 1 : 2 * pair + 2]], axis=1)

        onehot[:, lanes] = jnp.where(cell_index == row(target), 1.0, 0.0).astype(BF16)
        value_x, slope_x = [[row(x) for x in part] for part in polys[0]]
        value_y, slope_y = [pick([row(x) for x in part], node_row >> 2) for part in polys[1]]
        value_z, slope_z = [pick([row(x) for x in part], node_row & 3) for part in polys[2]]
        plain, along_y, along_z = value_y * value_z, slope_y * value_z, value_y * slope_z
        for a in range(4):
            at = slice(a * 16, a * 16 + 16)
            shapes[0, at, lanes] = value_x[a] * plain
            shapes[1, at, lanes] = slope_x[a] * plain
            shapes[2, at, lanes] = value_x[a] * along_y
            shapes[3, at, lanes] = value_x[a] * along_z
        gathered = dot(halves[...], onehot[:, lanes])
        for k in range(3):
            nodes = gathered[k * 64 : k * 64 + 64] + gathered[192 + k * 64 : 192 + k * 64 + 64]
            for j in range(4):
                total = jnp.sum(nodes * shapes[j, :, lanes], axis=0, keepdims=True)
                line = (k * 4 + j) * 8 + 2 * pair
                results[line : line + 1, :] = total[:, :128]
                results[line + 1 : line + 2, :] = total[:, 128:]

    own_visc = visc[...]
    visc_row = jnp.concatenate([own_visc[y : y + 1] for y in range(4)], axis=1)
    stiff = stiffness().astype(BF16)
    stiff = jnp.concatenate([stiff, stiff], axis=1)
    node = iota((64, 512), 0)
    ends = jnp.zeros((64, 512), F32)
    for step in (16, 4, 1):
        place = (node // step) % 4
        ends = ends + jnp.where((place == 0) | (place == 3), PENALTY, 0.0)
    for k in range(3):
        both = jnp.concatenate([halves[k * 64 : k * 64 + 64], halves[192 + k * 64 : 192 + k * 64 + 64]], axis=0)
        own = field[k].reshape(64, 512)
        applied[k] = (own * (1.0 + ends) + visc_row * dot(stiff, both)).reshape(4, 16, 512)

    arrive(second)
    mine = arrived[...].reshape(128, 128).T
    turned[...] = mine
    strain = [turned[pl.ds(r, 8, stride=16), :] for r in range(9)]
    motion = [turned[pl.ds(9 + r, 8, stride=16), :] for r in range(3)]
    seen = [results[q * 8 : q * 8 + 8, :] for q in range(12)]
    form = [[strain[k * 3 + l] + (1.0 if k == l else 0.0) for l in range(3)] for k in range(3)]
    moved = [
        [
            form[k][l]
            + TIME_STEP * (seen[k * 4 + 1] * form[0][l] + seen[k * 4 + 2] * form[1][l] + seen[k * 4 + 3] * form[2][l])
            for l in range(3)
        ]
        for k in range(3)
    ]
    for k in range(3):
        for l in range(3):
            reply_turned[pl.ds(k * 3 + l, 8, stride=16), :] = moved[k][l]
    reply[...] = reply_turned[...].T.reshape(16, 8, 128)
    third = over_solid(reply, reply_middle, send_c, recv_c, own_sem.at[2])
    start(third)

    stress = {}
    for k in range(3):
        for m in range(k, 3):
            value = moved[k][0] * moved[m][0] + moved[k][1] * moved[m][1] + moved[k][2] * moved[m][2]
            stress[k, m] = stress[m, k] = value - 1.0 if k == m else value
    drag = [SPRING_RATE * (motion[k] - seen[k * 4]) for k in range(3)]
    for pair in range(4):
        lanes = slice(pair * 256, pair * 256 + 256)

        def row(x):
            return jnp.concatenate([x[2 * pair : 2 * pair + 1], x[2 * pair + 1 : 2 * pair + 2]], axis=1)

        for k in range(3):
            node_force = row(drag[k]) * shapes[0, :, lanes]
            for j in range(3):
                node_force = node_force - row(stress[k, j]) * shapes[1 + j, :, lanes]
            high, low = split(node_force)
            nodal[k * 64 : k * 64 + 64, lanes] = high
            nodal[192 + k * 64 : 192 + k * 64 + 64, lanes] = low

    arrive(third)
    fourth = over_dy(reply_middle, reply_arrived, send_d, recv_d, own_sem.at[3])
    start(fourth)

    force = dot_nt(nodal[...], onehot[...])
    for copy in halo:
        copy.wait_recv()
    flipped = left_operand(jnp.concatenate([offsets[w].T for w in range(8)], axis=0))
    edge_lane = iota((32, 512), 1)
    edge_line = iota((32, 512), 0)
    edge_place = jnp.where(
        (edge_lane == (edge_line & 7) * 128 + jnp.where((edge_line & 8) == 0, 0, 127)) & ((edge_line & 7) < 4), 1.0, 0.0
    ).astype(BF16)
    below = jnp.where(me_s > 0, low_z[...], 0.0)
    above = jnp.where(me_s < N_SOLID - 1, high_z[...], 0.0)
    edge_high, edge_low = split(jnp.concatenate([below, above], axis=0).T)
    beside = dot(jnp.concatenate([edge_high, edge_low], axis=1), edge_place)
    lane = iota((64, 512), 1) & 127
    place_z = iota((64, 512), 0) & 3
    half_row = iota((4, 8, 512), 1)
    for k in range(3):
        own = field[k]
        flat = own.reshape(64, 512)
        outer = beside[k * 64 : k * 64 + 64]
        previous = jnp.concatenate([pltpu.roll(flat[:, y * 128 : y * 128 + 128], 1, 1) for y in range(4)], axis=1)
        following = jnp.concatenate([pltpu.roll(flat[:, y * 128 : y * 128 + 128], 127, 1) for y in range(4)], axis=1)
        previous = jnp.where(lane == 0, outer, previous)
        following = jnp.where(lane == 127, outer, following)
        near = jnp.where(place_z == 0, pltpu.roll(previous, 61, 0), 0.0)
        near = near + jnp.where(place_z == 3, pltpu.roll(following, 3, 0), 0.0)
        near = near.reshape(4, 16, 512)
        lower = jnp.concatenate([jnp.where(me_y > 0, low_y[k], 0.0), own[:, 8:16, :384]], axis=2)
        upper = jnp.concatenate([own[:, 0:8, 128:], jnp.where(me_y < N_DY - 1, high_y[k], 0.0)], axis=2)
        lower = jnp.where(half_row < 4, pltpu.roll(lower, 4, 1), 0.0)
        upper = jnp.where(half_row >= 4, pltpu.roll(upper, 4, 1), 0.0)
        near = near + jnp.concatenate([lower, upper], axis=1)
        lower = jnp.where(me_x > 0, low_x[k], 0.0)[None]
        upper = jnp.where(me_x < N_DX - 1, high_x[k], 0.0)[None]
        near = near + jnp.concatenate([lower, jnp.zeros((2, 16, 512), F32), upper], axis=0)
        total = (applied[k] - PENALTY * near).reshape(64, 512)
        total = total - force[k * 64 : k * 64 + 64] - force[192 + k * 64 : 192 + k * 64 + 64]
        result = constrain(total, flipped, config_row)
        for y in range(4):
            fluid[pl.ds(k * 256 + y, 64, stride=4), :] = result[:, y * 128 : y * 128 + 128]
    fluid_out = pltpu.make_async_copy(fluid, fluid_hbm, out_sem.at[0])
    fluid_out.start()

    device_slot = jnp.where((iota((256, 1024), 1) >> 3) == (iota((256, 1024), 0) & 127), 1.0, 0.0).astype(BF16)
    arrive(fourth)
    back_high, back_low = split(reply_arrived[...].reshape(128, 128).T)
    wide = dot(jnp.concatenate([back_high, back_low], axis=1), device_slot)
    slots = jnp.zeros((16, 1024), F32)
    for c in range(8):
        slots = slots + jnp.where(slot_place == c, wide[c * 16 : c * 16 + 16], 0.0)
    for g in range(8):
        deform[pl.ds(g, 16, stride=8), :] = slots[:, g * 128 : g * 128 + 128]
    deform_out = pltpu.make_async_copy(deform.at[0:72], deform_hbm, out_sem.at[1])
    deform_out.start()
    for copies in (first, second, third, fourth):
        for copy in copies[1:]:
            copy.wait_send()
    for copy in halo:
        copy.wait_send()
    fluid_out.wait()
    deform_out.wait()


def shards(velocity, viscosity, cell_config, constraint_offsets, slot_cells, point_coords, strain_offsets, solid_velocity):
    anywhere = pl.BlockSpec(memory_space=pl.ANY)
    vmem = pltpu.VMEM
    dma = pltpu.SemaphoreType.DMA
    fluid, deform = pl.pallas_call(
        kernel,
        out_shape=(jax.ShapeDtypeStruct((768, 128), F32), jax.ShapeDtypeStruct((72, 128), F32)),
        in_specs=[anywhere] * 8,
        out_specs=(anywhere, anywhere),
        scratch_shapes=[
            vmem((768, 128), F32),
            vmem((4, 128), F32),
            vmem((4, 128), jnp.int32),
            vmem((8, 64, 64), F32),
            vmem((8, 128), jnp.int32),
            vmem((128, 128), F32),
            vmem((3, 4, 16, 512), F32),
            vmem((384, 512), BF16),
            vmem((3, 4, 16, 512), F32),
            vmem((512, 1024), BF16),
            vmem((4, 64, 1024), F32),
            vmem((384, 1024), BF16),
            vmem((96, 128), F32),
            vmem((128, 128), F32),
            vmem((16, 8, 128), F32),
            vmem((16, 8, 128), F32),
            vmem((16, 8, 128), F32),
            vmem((16, 8, 128), F32),
            vmem((16, 8, 128), F32),
            vmem((16, 8, 128), F32),
            vmem((128, 128), F32),
            vmem((2, 8, 192), F32),
            vmem((3, 16, 512), F32),
            vmem((3, 16, 512), F32),
            vmem((3, 4, 8, 128), F32),
            vmem((3, 4, 8, 128), F32),
            vmem((8, 192), F32),
            vmem((8, 192), F32),
            vmem((768, 128), F32),
            vmem((128, 128), F32),
            dma((8,)),
            dma((4,)),
            dma((2,)),
            dma((N_SOLID - 1,)),
            dma((N_SOLID - 1,)),
            dma((N_DY - 1,)),
            dma((N_DY - 1,)),
            dma((N_SOLID - 1,)),
            dma((N_SOLID - 1,)),
            dma((N_DY - 1,)),
            dma((N_DY - 1,)),
            dma((6,)),
            dma((6,)),
        ],
        compiler_params=pltpu.CompilerParams(collective_id=0, has_side_effects=True),
    )(
        velocity.reshape(768, 128),
        viscosity.reshape(4, 128),
        cell_config.reshape(4, 128),
        constraint_offsets,
        slot_cells.reshape(8, 128),
        point_coords.reshape(24, 128),
        strain_offsets.reshape(72, 128),
        solid_velocity.reshape(24, 128),
    )
    return fluid.reshape(velocity.shape), deform.reshape(strain_offsets.shape)


def solution(mesh):
    return jax.shard_map(
        shards,
        mesh=mesh,
        in_specs=(
            P(None, None, None, None, "dx", "dy", "solid"),
            P("dx", "dy", "solid"),
            P("dx", "dy", "solid"),
            P(),
            P("dx", ("dy", "solid"), None),
            P(None, "dx", ("dy", "solid"), None),
            P(None, None, "dx", ("dy", "solid"), None),
            P(None, "dx", ("dy", "solid"), None),
        ),
        out_specs=(
            P(None, None, None, None, "dx", "dy", "solid"),
            P(None, None, "dx", ("dy", "solid"), None),
        ),
        check_vma=False,
    )
```

time: 203 us -> 39 us (0.19); the launches traced: 200 us -> 38.8 us
  local copies, waits for them, and re-layouts: 59.2 us -> 2.39 us
  starting transfers between devices: 52.5 us -> 0 us
  Pallas kernels: 0 us -> 35.8 us
  waiting for transfers between devices: 32.7 us -> 0 us
  matrix products: 32.4 us -> 0 us
  other arithmetic: 21.4 us -> 0 us
    all_to_all x2 -> x0, starting transfers between devices: 36.7 us -> none  [the longest x1 29.6 us: shards(): lax.all_to_all(packed, ('dy', 'solid'), split_axis=1, concat_axis=1, tile...]
    pallas_call x0 -> x1, Pallas kernels: none -> 35.8 us  [shards(): pl.pallas_call(kernel, out_shape=(jax.ShapeDtypeStruct((768, 128), F32),...]
    dot_general x21 -> x0, matrix products: 32.4 us -> none  [the longest x1 9.88 us: solid_update(): jnp.einsum('kjs,jls->kls', grad, deform, precision=PRECISE)]
    all_to_all x2 -> x0, waiting for transfers between devices: 29.8 us -> none  [the longest x1 16.6 us: shards(): lax.all_to_all(reply, ('dy', 'solid'), split_axis=1, concat_axis=1, tiled...]
    slice x9 -> x0, local copies, waits for them, and re-layouts: 16.1 us -> none  [the longest x3 7.1 us: extended(): initial = lax.slice_in_dim(shard, 0, width, axis=dim)]
    ppermute x6 -> x0, starting transfers between devices: 15.8 us -> none  [the longest x3 11.2 us: extended(): before = lax.ppermute(last, axis, up)]
    scatter-add x5 -> x0, other arithmetic: 10.8 us -> none  [the longest x1 6.3 us: shards(): force = jnp.zeros_like(block).at[:, safe].add(nodal)]
    ppermute x2 -> x0, local copies, waits for them, and re-layouts: 10.3 us -> none  [the longest x1 5.59 us: extended(): after = lax.ppermute(initial, axis, down)]
  transfers between devices with their start and end apart: 8 -> 0, of which waited for: 3 -> 0; matrix products, arithmetic and copies ran while one was open for 39% -> 0% of each run, Pallas kernels for 0% -> 0%
where the time goes in v1:
time: 39 us; the launch traced here: 38.8 us
  Pallas kernels  35.8 us (92%)
  local copies, waits for them, and re-layouts  2.39 us (6%)
  between operations  0.65 us (2%)
    pallas_call x1, Pallas kernels, shards(): pl.pallas_call(kernel, out_shape=(jax.ShapeDtypeStruct((768, 128), F32),...  35.8 us
    unnamed x4, local copies, waits for them, and re-layouts  2.39 us

profile of v1, /device:TPU:1, one launch (start us, length us, event | category | flops | bytes accessed | tf_op | source)
XLA Modules:
  0.0 38.8 jit_solution(18268020669599369257)
XLA Ops:
  0.6 35.8 %shard_map.95 = (f32[768,128]{1,0:T(8,128)}, f32[72,128]{1,0:T(8,128)}) custom-call(f32[768,128]{1,0:T(8,128)} %bitcast.11, f32[4,128]{1,0:T(4,128)} %bitcast.18, s32[4,128]{1,0:T(4,128)} %bitcast.19, f32[8,64,64]{2,1,0:T(8,128)} %offsets_hbm.1, s32[8,128]{1,0:T(8,128)} %bitcast.17, f32[24,128]{1,0:T(8,128)} %bitcast.15, f32[72,128]{1,0:T(8,128)} %bitcast.13, ...), custom_call_target="tpu_custom_call" | custom-call | tf_op jit(solution)/shard_map/pallas_call | solution.py:380
  36.4 0.0 copy-start
  36.4 1.8 %copy.16 = f32[3,4,4,4,1,4,128]{6,5,4,3,2,1,0:T(4,128)} copy(f32[3,4,4,4,1,4,128]{6,5,4,3,2,1,0:T(4,128)} %bitcast.12) | data formatting | bytes 786432
  38.2 0.0 copy-done
  38.2 0.6 %copy.17 = f32[3,3,1,1,1024]{4,3,2,1,0:T(1,128)} copy(f32[3,3,1,1,1024]{4,3,2,1,0:T(1,128)S(1)} %bitcast.14) | data formatting | bytes 73728
Async XLA Ops:
  36.4 1.8 %copy-start = (f32[72,128]{1,0:T(8,128)S(1)}, f32[72,128]{1,0:T(8,128)}, u32[]{:S(2)}) copy-start(f32[72,128]{1,0:T(8,128)} %get-tuple-element.5) | copy-start | bytes 110596

commit v2 on v1

--- a/solution.py
+++ b/solution.py
@@ -54,6 +54,18 @@
     return jnp.where(index < 2, out, jnp.where(index == 2, rows[2], rows[3]))
 
 
+def deformed(strain, grad):
+    form = [[strain[k * 3 + l] + (1.0 if k == l else 0.0) for l in range(3)] for k in range(3)]
+    return [
+        [
+            form[k][l]
+            + TIME_STEP * (grad[k * 3] * form[0][l] + grad[k * 3 + 1] * form[1][l] + grad[k * 3 + 2] * form[2][l])
+            for l in range(3)
+        ]
+        for k in range(3)
+    ]
+
+
 def stiffness():
     row, col = iota((64, 64), 0), iota((64, 64), 1)
     total = jnp.where(row == col, 6.0, 0.0)
@@ -81,16 +93,23 @@
 
 def kernel(
     vel_hbm, visc_hbm, config_hbm, offsets_hbm, cells_hbm, coords_hbm, strain_hbm, motion_hbm,
-    fluid_hbm, deform_hbm,
+    fluid, deform,
     vel, visc, config, offsets, cells, items,
-    field, halves, applied, onehot, shapes, nodal, results, turned,
+    field, halves, applied, onehot, shapes, nodal, results, turned, grads,
     packet, middle, arrived, reply, reply_middle, reply_arrived, reply_turned,
     edge, low_x, high_x, low_y, high_y, low_z, high_z,
-    fluid, deform,
-    in_sem, own_sem, out_sem,
+    in_sem, own_sem,
     send_a, recv_a, send_b, recv_b, send_c, recv_c, send_d, recv_d, send_h, recv_h,
 ):
     me_x, me_y, me_s = lax.axis_index("dx"), lax.axis_index("dy"), lax.axis_index("solid")
+
+    barrier = pltpu.get_barrier_semaphore()
+    for step in range(1, N_SOLID):
+        pl.semaphore_signal(barrier, inc=1, device_id={"solid": lax.rem(me_s + step, N_SOLID)}, device_id_type=MESH)
+    for step in range(1, N_DY):
+        pl.semaphore_signal(barrier, inc=1, device_id={"dy": lax.rem(me_y + step, N_DY)}, device_id_type=MESH)
+    for step in (1, N_DX - 1):
+        pl.semaphore_signal(barrier, inc=1, device_id={"dx": lax.rem(me_x + step, N_DX)}, device_id_type=MESH)
 
     loads = [
         pltpu.make_async_copy(source, target, in_sem.at[which])
@@ -110,14 +129,6 @@
     for load in loads:
         load.start()
 
-    barrier = pltpu.get_barrier_semaphore()
-    for step in range(1, N_SOLID):
-        pl.semaphore_signal(barrier, inc=1, device_id={"solid": lax.rem(me_s + step, N_SOLID)}, device_id_type=MESH)
-    for step in range(1, N_DY):
-        pl.semaphore_signal(barrier, inc=1, device_id={"dy": lax.rem(me_y + step, N_DY)}, device_id_type=MESH)
-    for step in (1, N_DX - 1):
-        pl.semaphore_signal(barrier, inc=1, device_id={"dx": lax.rem(me_x + step, N_DX)}, device_id_type=MESH)
-
     def over_solid(source, target, send, recv, own):
         copies = [pltpu.make_async_copy(source.at[:, me_s], target.at[:, me_s], own)]
         for step in range(1, N_SOLID):
@@ -173,7 +184,7 @@
     reply_turned[...] = jnp.zeros_like(reply_turned)
 
     pl.semaphore_wait(barrier, N_SOLID - 1 + N_DY - 1 + 2)
-    first = over_solid(packet, middle, send_a, recv_a, own_sem.at[0])
+    first = over_dy(packet, middle, send_a, recv_a, own_sem.at[0])
     start(first)
 
     for load in loads[4:]:
@@ -188,36 +199,6 @@
         high, low = split(own)
         halves[k * 64 : k * 64 + 64] = high
         halves[192 + k * 64 : 192 + k * 64 + 64] = low
-
-    def remote(source, target, which, where):
-        return pltpu.make_async_remote_copy(
-            src_ref=source, dst_ref=target, send_sem=send_h.at[which], recv_sem=recv_h.at[which],
-            device_id=where, device_id_type=MESH,
-        )
-
-    up_x, down_x = lax.rem(me_x + 1, N_DX), lax.rem(me_x + N_DX - 1, N_DX)
-    up_y, down_y = lax.rem(me_y + 1, N_DY), lax.rem(me_y + N_DY - 1, N_DY)
-    up_s, down_s = lax.rem(me_s + 1, N_SOLID), lax.rem(me_s + N_SOLID - 1, N_SOLID)
-    halo = [
-        remote(field.at[:, 3], low_x, 0, {"dx": up_x}),
-        remote(field.at[:, 0], high_x, 1, {"dx": down_x}),
-        remote(field.at[:, :, 8:16, 384:512], low_y, 2, {"dy": up_y}),
-        remote(field.at[:, :, 0:8, 0:128], high_y, 3, {"dy": down_y}),
-        remote(edge.at[0], low_z, 4, {"solid": up_s}),
-        remote(edge.at[1], high_z, 5, {"solid": down_s}),
-    ]
-    edge_row, edge_col = iota((16, 512), 0), iota((16, 512), 1)
-    lane_edge = jnp.where(edge_row < 8, 127, 0)
-    edge_pick = jnp.where(
-        (edge_col == (edge_row & 7) * 128 + lane_edge) & ((edge_row & 7) < 4), 1.0, 0.0
-    ).astype(BF16)
-    edges = dot_nt(edge_pick, halves[0:192]) + dot_nt(edge_pick, halves[192:384])
-    edge[...] = edges.reshape(2, 8, 192)
-
-    arrive(first)
-    second = over_dy(middle, arrived, send_b, recv_b, own_sem.at[1])
-    start(second)
-    start(halo)
 
     points = [turned[pl.ds(12 + j, 8, stride=16), :] for j in range(3)]
     target = turned[pl.ds(15, 8, stride=16), :]
@@ -249,6 +230,39 @@
                 line = (k * 4 + j) * 8 + 2 * pair
                 results[line : line + 1, :] = total[:, :128]
                 results[line + 1 : line + 2, :] = total[:, 128:]
+    seen = [results[q * 8 : q * 8 + 8, :] for q in range(12)]
+    for k in range(3):
+        for j in range(3):
+            reply_turned[pl.ds(k * 3 + j, 8, stride=16), :] = seen[k * 4 + 1 + j]
+    reply[...] = reply_turned[...].T.reshape(16, 8, 128)
+    second = over_dy(reply, reply_middle, send_c, recv_c, own_sem.at[2])
+    start(second)
+
+    def remote(source, target, which, where):
+        return pltpu.make_async_remote_copy(
+            src_ref=source, dst_ref=target, send_sem=send_h.at[which], recv_sem=recv_h.at[which],
+            device_id=where, device_id_type=MESH,
+        )
+
+    up_x, down_x = lax.rem(me_x + 1, N_DX), lax.rem(me_x + N_DX - 1, N_DX)
+    up_y, down_y = lax.rem(me_y + 1, N_DY), lax.rem(me_y + N_DY - 1, N_DY)
+    up_s, down_s = lax.rem(me_s + 1, N_SOLID), lax.rem(me_s + N_SOLID - 1, N_SOLID)
+    halo = [
+        remote(field.at[:, 3], low_x, 0, {"dx": up_x}),
+        remote(field.at[:, 0], high_x, 1, {"dx": down_x}),
+        remote(field.at[:, :, 8:16, 384:512], low_y, 2, {"dy": up_y}),
+        remote(field.at[:, :, 0:8, 0:128], high_y, 3, {"dy": down_y}),
+        remote(edge.at[0], low_z, 4, {"solid": up_s}),
+        remote(edge.at[1], high_z, 5, {"solid": down_s}),
+    ]
+    edge_row, edge_col = iota((16, 512), 0), iota((16, 512), 1)
+    lane_edge = jnp.where(edge_row < 8, 127, 0)
+    edge_pick = jnp.where(
+        (edge_col == (edge_row & 7) * 128 + lane_edge) & ((edge_row & 7) < 4), 1.0, 0.0
+    ).astype(BF16)
+    edges = dot_nt(edge_pick, halves[0:192]) + dot_nt(edge_pick, halves[192:384])
+    edge[...] = edges.reshape(2, 8, 192)
+    start(halo)
 
     own_visc = visc[...]
     visc_row = jnp.concatenate([own_visc[y : y + 1] for y in range(4)], axis=1)
@@ -264,53 +278,13 @@
         own = field[k].reshape(64, 512)
         applied[k] = (own * (1.0 + ends) + visc_row * dot(stiff, both)).reshape(4, 16, 512)
 
+    arrive(first)
+    third = over_solid(middle, arrived, send_b, recv_b, own_sem.at[1])
+    start(third)
     arrive(second)
-    mine = arrived[...].reshape(128, 128).T
-    turned[...] = mine
-    strain = [turned[pl.ds(r, 8, stride=16), :] for r in range(9)]
-    motion = [turned[pl.ds(9 + r, 8, stride=16), :] for r in range(3)]
-    seen = [results[q * 8 : q * 8 + 8, :] for q in range(12)]
-    form = [[strain[k * 3 + l] + (1.0 if k == l else 0.0) for l in range(3)] for k in range(3)]
-    moved = [
-        [
-            form[k][l]
-            + TIME_STEP * (seen[k * 4 + 1] * form[0][l] + seen[k * 4 + 2] * form[1][l] + seen[k * 4 + 3] * form[2][l])
-            for l in range(3)
-        ]
-        for k in range(3)
-    ]
-    for k in range(3):
-        for l in range(3):
-            reply_turned[pl.ds(k * 3 + l, 8, stride=16), :] = moved[k][l]
-    reply[...] = reply_turned[...].T.reshape(16, 8, 128)
-    third = over_solid(reply, reply_middle, send_c, recv_c, own_sem.at[2])
-    start(third)
-
-    stress = {}
-    for k in range(3):
-        for m in range(k, 3):
-            value = moved[k][0] * moved[m][0] + moved[k][1] * moved[m][1] + moved[k][2] * moved[m][2]
-            stress[k, m] = stress[m, k] = value - 1.0 if k == m else value
-    drag = [SPRING_RATE * (motion[k] - seen[k * 4]) for k in range(3)]
-    for pair in range(4):
-        lanes = slice(pair * 256, pair * 256 + 256)
-
-        def row(x):
-            return jnp.concatenate([x[2 * pair : 2 * pair + 1], x[2 * pair + 1 : 2 * pair + 2]], axis=1)
-
-        for k in range(3):
-            node_force = row(drag[k]) * shapes[0, :, lanes]
-            for j in range(3):
-                node_force = node_force - row(stress[k, j]) * shapes[1 + j, :, lanes]
-            high, low = split(node_force)
-            nodal[k * 64 : k * 64 + 64, lanes] = high
-            nodal[192 + k * 64 : 192 + k * 64 + 64, lanes] = low
-
-    arrive(third)
-    fourth = over_dy(reply_middle, reply_arrived, send_d, recv_d, own_sem.at[3])
+    fourth = over_solid(reply_middle, reply_arrived, send_d, recv_d, own_sem.at[3])
     start(fourth)
 
-    force = dot_nt(nodal[...], onehot[...])
     for copy in halo:
         copy.wait_recv()
     flipped = left_operand(jnp.concatenate([offsets[w].T for w in range(8)], axis=0))
@@ -345,15 +319,43 @@
         lower = jnp.where(me_x > 0, low_x[k], 0.0)[None]
         upper = jnp.where(me_x < N_DX - 1, high_x[k], 0.0)[None]
         near = near + jnp.concatenate([lower, jnp.zeros((2, 16, 512), F32), upper], axis=0)
-        total = (applied[k] - PENALTY * near).reshape(64, 512)
+        applied[k] = applied[k] - PENALTY * near
+    device_slot = jnp.where((iota((256, 1024), 1) >> 3) == (iota((256, 1024), 0) & 127), 1.0, 0.0).astype(BF16)
+
+    arrive(third)
+    turned[...] = arrived[...].reshape(128, 128).T
+    moved = deformed(
+        [turned[pl.ds(r, 8, stride=16), :] for r in range(9)],
+        [seen[k * 4 + 1 + j] for k in range(3) for j in range(3)],
+    )
+    motion = [turned[pl.ds(9 + r, 8, stride=16), :] for r in range(3)]
+    stress = {}
+    for k in range(3):
+        for m in range(k, 3):
+            value = moved[k][0] * moved[m][0] + moved[k][1] * moved[m][1] + moved[k][2] * moved[m][2]
+            stress[k, m] = stress[m, k] = value - 1.0 if k == m else value
+    drag = [SPRING_RATE * (motion[k] - seen[k * 4]) for k in range(3)]
+    for pair in range(4):
+        lanes = slice(pair * 256, pair * 256 + 256)
+
+        def row(x):
+            return jnp.concatenate([x[2 * pair : 2 * pair + 1], x[2 * pair + 1 : 2 * pair + 2]], axis=1)
+
+        for k in range(3):
+            node_force = row(drag[k]) * shapes[0, :, lanes]
+            for j in range(3):
+                node_force = node_force - row(stress[k, j]) * shapes[1 + j, :, lanes]
+            high, low = split(node_force)
+            nodal[k * 64 : k * 64 + 64, lanes] = high
+            nodal[192 + k * 64 : 192 + k * 64 + 64, lanes] = low
+    force = dot_nt(nodal[...], onehot[...])
+    for k in range(3):
+        total = applied[k].reshape(64, 512)
         total = total - force[k * 64 : k * 64 + 64] - force[192 + k * 64 : 192 + k * 64 + 64]
         result = constrain(total, flipped, config_row)
         for y in range(4):
             fluid[pl.ds(k * 256 + y, 64, stride=4), :] = result[:, y * 128 : y * 128 + 128]
-    fluid_out = pltpu.make_async_copy(fluid, fluid_hbm, out_sem.at[0])
-    fluid_out.start()
-
-    device_slot = jnp.where((iota((256, 1024), 1) >> 3) == (iota((256, 1024), 0) & 127), 1.0, 0.0).astype(BF16)
+
     arrive(fourth)
     back_high, back_low = split(reply_arrived[...].reshape(128, 128).T)
     wide = dot(jnp.concatenate([back_high, back_low], axis=1), device_slot)
@@ -361,27 +363,31 @@
     for c in range(8):
         slots = slots + jnp.where(slot_place == c, wide[c * 16 : c * 16 + 16], 0.0)
     for g in range(8):
-        deform[pl.ds(g, 16, stride=8), :] = slots[:, g * 128 : g * 128 + 128]
-    deform_out = pltpu.make_async_copy(deform.at[0:72], deform_hbm, out_sem.at[1])
-    deform_out.start()
+        grads[pl.ds(g, 16, stride=8), :] = slots[:, g * 128 : g * 128 + 128]
+    moved = deformed(
+        [items[r * 8 : r * 8 + 8, :] for r in range(9)],
+        [grads[r * 8 : r * 8 + 8, :] for r in range(9)],
+    )
+    for k in range(3):
+        for l in range(3):
+            deform[(k * 3 + l) * 8 : (k * 3 + l) * 8 + 8, :] = moved[k][l]
     for copies in (first, second, third, fourth):
         for copy in copies[1:]:
             copy.wait_send()
     for copy in halo:
         copy.wait_send()
-    fluid_out.wait()
-    deform_out.wait()
 
 
 def shards(velocity, viscosity, cell_config, constraint_offsets, slot_cells, point_coords, strain_offsets, solid_velocity):
     anywhere = pl.BlockSpec(memory_space=pl.ANY)
+    inside = pl.BlockSpec(memory_space=pltpu.VMEM)
     vmem = pltpu.VMEM
     dma = pltpu.SemaphoreType.DMA
     fluid, deform = pl.pallas_call(
         kernel,
-        out_shape=(jax.ShapeDtypeStruct((768, 128), F32), jax.ShapeDtypeStruct((72, 128), F32)),
+        out_shape=(vmem((768, 128), F32), vmem((72, 128), F32)),
         in_specs=[anywhere] * 8,
-        out_specs=(anywhere, anywhere),
+        out_specs=(inside, inside),
         scratch_shapes=[
             vmem((768, 128), F32),
             vmem((4, 128), F32),
@@ -397,6 +403,7 @@
             vmem((384, 1024), BF16),
             vmem((96, 128), F32),
             vmem((128, 128), F32),
+            vmem((128, 128), F32),
             vmem((16, 8, 128), F32),
             vmem((16, 8, 128), F32),
             vmem((16, 8, 128), F32),
@@ -411,19 +418,16 @@
             vmem((3, 4, 8, 128), F32),
             vmem((8, 192), F32),
             vmem((8, 192), F32),
-            vmem((768, 128), F32),
-            vmem((128, 128), F32),
             dma((8,)),
             dma((4,)),
-            dma((2,)),
+            dma((N_DY - 1,)),
+            dma((N_DY - 1,)),
             dma((N_SOLID - 1,)),
             dma((N_SOLID - 1,)),
             dma((N_DY - 1,)),
             dma((N_DY - 1,)),
             dma((N_SOLID - 1,)),
             dma((N_SOLID - 1,)),
-            dma((N_DY - 1,)),
-            dma((N_DY - 1,)),
             dma((6,)),
             dma((6,)),
         ],

time: 39 us -> 29.7 us (0.76)
  Pallas kernels: 35.8 us -> 27.6 us
  local copies, waits for them, and re-layouts: 2.39 us -> 1.36 us
    pallas_call x1, Pallas kernels: 35.8 us -> 27.6 us  [shards(): pl.pallas_call(kernel, out_shape=(vmem((768, 128), F32), vmem((72, 128),...]
    unnamed x4 -> x2, local copies, waits for them, and re-layouts: 2.39 us -> 1.36 us
where the time goes in v2:
time: 29.7 us; the launch traced here: 29.6 us
  Pallas kernels  27.6 us (93%)
  local copies, waits for them, and re-layouts  1.36 us (5%)
  between operations  0.64 us (2%)
    pallas_call x1, Pallas kernels, shards(): pl.pallas_call(kernel, out_shape=(vmem((768, 128), F32), vmem((72, 128),...  27.6 us
    unnamed x2, local copies, waits for them, and re-layouts  1.36 us

profile of v2, /device:TPU:1, one launch (start us, length us, event | category | flops | bytes accessed | tf_op | source)
XLA Modules:
  0.0 29.6 jit_solution(15701392284090648895)
XLA Ops:
  0.6 27.6 %shard_map.95 = (f32[768,128]{1,0:T(8,128)S(1)}, f32[72,128]{1,0:T(8,128)S(1)}) custom-call(f32[768,128]{1,0:T(8,128)} %bitcast.13, f32[4,128]{1,0:T(4,128)} %bitcast.18, s32[4,128]{1,0:T(4,128)} %bitcast.19, f32[8,64,64]{2,1,0:T(8,128)} %offsets_hbm.1, s32[8,128]{1,0:T(8,128)} %bitcast.17, f32[24,128]{1,0:T(8,128)} %bitcast.15, f32[72,128]{1,0:T(8,128)} %bitcast.14, ...), custom_call_target="tpu_custom_call" | custom-call | tf_op jit(solution)/shard_map/pallas_call | solution.py:386
  28.2 0.7 %copy.16 = f32[3,4,4,4,1,4,128]{6,5,4,3,2,1,0:T(4,128)} copy(f32[3,4,4,4,1,4,128]{6,5,4,3,2,1,0:T(4,128)S(1)} %bitcast.11) | data formatting | bytes 786432
  28.9 0.6 %copy.17 = f32[3,3,1,1,1024]{4,3,2,1,0:T(1,128)} copy(f32[3,3,1,1,1024]{4,3,2,1,0:T(1,128)S(1)} %bitcast.12) | data formatting | bytes 73728

commit v3 on v2

--- a/solution.py
+++ b/solution.py
@@ -98,16 +98,30 @@
     field, halves, applied, onehot, shapes, nodal, results, turned, grads,
     packet, middle, arrived, reply, reply_middle, reply_arrived, reply_turned,
     edge, low_x, high_x, low_y, high_y, low_z, high_z,
-    in_sem, own_sem,
+    in_sem, own_sem, entered_y, entered_s,
     send_a, recv_a, send_b, recv_b, send_c, recv_c, send_d, recv_d, send_h, recv_h,
 ):
     me_x, me_y, me_s = lax.axis_index("dx"), lax.axis_index("dy"), lax.axis_index("solid")
 
+    def rank(place):
+        return jnp.where(place < 4, place, 11 - place)
+
+    def later_s(step):
+        return rank(lax.rem(me_s + step, N_SOLID)) > rank(me_s)
+
     barrier = pltpu.get_barrier_semaphore()
+    for step in range(1, N_DY):
+
+        @pl.when(me_y + step < N_DY)
+        def _():
+            pl.semaphore_signal(barrier, inc=1, device_id={"dy": me_y + step}, device_id_type=MESH)
+
     for step in range(1, N_SOLID):
-        pl.semaphore_signal(barrier, inc=1, device_id={"solid": lax.rem(me_s + step, N_SOLID)}, device_id_type=MESH)
-    for step in range(1, N_DY):
-        pl.semaphore_signal(barrier, inc=1, device_id={"dy": lax.rem(me_y + step, N_DY)}, device_id_type=MESH)
+
+        @pl.when(later_s(step))
+        def _():
+            pl.semaphore_signal(barrier, inc=1, device_id={"solid": lax.rem(me_s + step, N_SOLID)}, device_id_type=MESH)
+
     for step in (1, N_DX - 1):
         pl.semaphore_signal(barrier, inc=1, device_id={"dx": lax.rem(me_x + step, N_DX)}, device_id_type=MESH)
 
@@ -165,6 +179,30 @@
         for copy in copies:
             copy.start()
 
+    def start_early(copies):
+        copies[0].start()
+        for step in range(1, N_DY):
+
+            @pl.when(me_y + step >= N_DY)
+            def _():
+                copies[step].start()
+
+    def start_late(groups):
+        for step in range(1, N_DY):
+
+            @pl.when(me_y + step < N_DY)
+            def _():
+                pl.semaphore_wait(entered_y.at[step - 1], 1)
+                for copies in groups:
+                    copies[step].start()
+
+    def greet_s():
+        for step in range(1, N_SOLID):
+
+            @pl.when(later_s(step))
+            def _():
+                pl.semaphore_wait(entered_s.at[step - 1], 1)
+
     def arrive(copies):
         copies[0].wait()
         for copy in copies[1:]:
@@ -183,9 +221,26 @@
     turned[...] = packed
     reply_turned[...] = jnp.zeros_like(reply_turned)
 
-    pl.semaphore_wait(barrier, N_SOLID - 1 + N_DY - 1 + 2)
+    pl.semaphore_wait(barrier, me_y + rank(me_s) + 2)
+    for step in range(1, N_DY):
+
+        @pl.when(me_y >= step)
+        def _():
+            pl.semaphore_signal(entered_y.at[step - 1], inc=1, device_id={"dy": me_y - step}, device_id_type=MESH)
+
+    for step in range(1, N_SOLID):
+
+        @pl.when(jnp.logical_not(later_s(step)))
+        def _():
+            pl.semaphore_signal(
+                entered_s.at[N_SOLID - 1 - step],
+                inc=1,
+                device_id={"solid": lax.rem(me_s + step, N_SOLID)},
+                device_id_type=MESH,
+            )
+
     first = over_dy(packet, middle, send_a, recv_a, own_sem.at[0])
-    start(first)
+    start_early(first)
 
     for load in loads[4:]:
         load.wait()
@@ -236,7 +291,9 @@
             reply_turned[pl.ds(k * 3 + j, 8, stride=16), :] = seen[k * 4 + 1 + j]
     reply[...] = reply_turned[...].T.reshape(16, 8, 128)
     second = over_dy(reply, reply_middle, send_c, recv_c, own_sem.at[2])
-    start(second)
+    start_early(second)
+    start_late([first, second])
+
 
     def remote(source, target, which, where):
         return pltpu.make_async_remote_copy(
@@ -255,6 +312,8 @@
         remote(edge.at[0], low_z, 4, {"solid": up_s}),
         remote(edge.at[1], high_z, 5, {"solid": down_s}),
     ]
+    start(halo[:4])
+    greet_s()
     edge_row, edge_col = iota((16, 512), 0), iota((16, 512), 1)
     lane_edge = jnp.where(edge_row < 8, 127, 0)
     edge_pick = jnp.where(
@@ -262,7 +321,7 @@
     ).astype(BF16)
     edges = dot_nt(edge_pick, halves[0:192]) + dot_nt(edge_pick, halves[192:384])
     edge[...] = edges.reshape(2, 8, 192)
-    start(halo)
+    start(halo[4:])
 
     own_visc = visc[...]
     visc_row = jnp.concatenate([own_visc[y : y + 1] for y in range(4)], axis=1)
@@ -376,6 +435,17 @@
             copy.wait_send()
     for copy in halo:
         copy.wait_send()
+
+
+def place_kernel(fluid, deform, fluid_hbm, deform_hbm, sem):
+    copies = [
+        pltpu.make_async_copy(fluid, fluid_hbm, sem.at[0]),
+        pltpu.make_async_copy(deform, deform_hbm, sem.at[1]),
+    ]
+    for copy in copies:
+        copy.start()
+    for copy in copies:
+        copy.wait()
 
 
 def shards(velocity, viscosity, cell_config, constraint_offsets, slot_cells, point_coords, strain_offsets, solid_velocity):
@@ -420,6 +490,8 @@
             vmem((8, 192), F32),
             dma((8,)),
             dma((4,)),
+            pltpu.SemaphoreType.REGULAR((N_DY - 1,)),
+            pltpu.SemaphoreType.REGULAR((N_SOLID - 1,)),
             dma((N_DY - 1,)),
             dma((N_DY - 1,)),
             dma((N_SOLID - 1,)),
@@ -442,6 +514,13 @@
         strain_offsets.reshape(72, 128),
         solid_velocity.reshape(24, 128),
     )
+    fluid, deform = pl.pallas_call(
+        place_kernel,
+        out_shape=(jax.ShapeDtypeStruct((768, 128), F32), jax.ShapeDtypeStruct((72, 128), F32)),
+        in_specs=[inside, inside],
+        out_specs=(anywhere, anywhere),
+        scratch_shapes=[dma((2,))],
+    )(pltpu.with_memory_space_constraint(fluid, pltpu.VMEM), pltpu.with_memory_space_constraint(deform, pltpu.VMEM))
     return fluid.reshape(velocity.shape), deform.reshape(strain_offsets.shape)
 
 

time: 29.7 us -> 28.3 us (0.953)
  local copies, waits for them, and re-layouts: 1.36 us -> 0 us
    unnamed x2 -> x0, local copies, waits for them, and re-layouts: 1.36 us -> none
    pallas_call x1, Pallas kernels: 27.6 us -> 26.7 us  [shards(): pl.pallas_call(kernel, out_shape=(vmem((768, 128), F32), vmem((72, 128),...]
    pallas_call x0 -> x1, Pallas kernels: none -> 0.77 us  [shards(): pl.pallas_call(place_kernel, out_shape=(jax.ShapeDtypeStruct((768, 128),...]
where the time goes in v3:
time: 28.3 us; the launch traced here: 28.1 us
  Pallas kernels  27.5 us (97%)
  between operations  0.64 us (2%)
    pallas_call x1, Pallas kernels, shards(): pl.pallas_call(kernel, out_shape=(vmem((768, 128), F32), vmem((72, 128),...  26.7 us
    pallas_call x1, Pallas kernels, shards(): pl.pallas_call(place_kernel, out_shape=(jax.ShapeDtypeStruct((768, 128),...  0.77 us

profile of v3, /device:TPU:1, one launch (start us, length us, event | category | flops | bytes accessed | tf_op | source)
XLA Modules:
  0.0 28.1 jit_solution(10057981865202845674)
XLA Ops:
  0.6 26.7 %shard_map.95 = (f32[768,128]{1,0:T(8,128)S(1)}, f32[72,128]{1,0:T(8,128)S(1)}) custom-call(f32[768,128]{1,0:T(8,128)} %bitcast.11, f32[4,128]{1,0:T(4,128)} %bitcast.16, s32[4,128]{1,0:T(4,128)} %bitcast.17, f32[8,64,64]{2,1,0:T(8,128)} %offsets_hbm.1, s32[8,128]{1,0:T(8,128)} %bitcast.15, f32[24,128]{1,0:T(8,128)} %bitcast.13, f32[72,128]{1,0:T(8,128)} %bitcast.12, ...), custom_call_target="tpu_custom_call" | custom-call | tf_op jit(solution)/shard_map/pallas_call | solution.py:456
  27.4 0.8 %shard_map.96 = (f32[768,128]{1,0:T(8,128)}, f32[72,128]{1,0:T(8,128)}) custom-call(f32[768,128]{1,0:T(8,128)S(1)} %get-tuple-element.6.fluid, f32[72,128]{1,0:T(8,128)S(1)} %get-tuple-element.7.deform), custom_call_target="tpu_custom_call" | custom-call | tf_op jit(solution)/shard_map/pallas_call | solution.py:517

commit v4 on v3

--- a/solution.py
+++ b/solution.py
@@ -95,35 +95,13 @@
     vel_hbm, visc_hbm, config_hbm, offsets_hbm, cells_hbm, coords_hbm, strain_hbm, motion_hbm,
     fluid, deform,
     vel, visc, config, offsets, cells, items,
-    field, halves, applied, onehot, shapes, nodal, results, turned, grads,
+    slot_device, field, halves, applied, onehot, shapes, nodal, results, turned, grads,
     packet, middle, arrived, reply, reply_middle, reply_arrived, reply_turned,
     edge, low_x, high_x, low_y, high_y, low_z, high_z,
-    in_sem, own_sem, entered_y, entered_s,
+    in_sem, own_sem, entered_x, entered_y, entered_s,
     send_a, recv_a, send_b, recv_b, send_c, recv_c, send_d, recv_d, send_h, recv_h,
 ):
     me_x, me_y, me_s = lax.axis_index("dx"), lax.axis_index("dy"), lax.axis_index("solid")
-
-    def rank(place):
-        return jnp.where(place < 4, place, 11 - place)
-
-    def later_s(step):
-        return rank(lax.rem(me_s + step, N_SOLID)) > rank(me_s)
-
-    barrier = pltpu.get_barrier_semaphore()
-    for step in range(1, N_DY):
-
-        @pl.when(me_y + step < N_DY)
-        def _():
-            pl.semaphore_signal(barrier, inc=1, device_id={"dy": me_y + step}, device_id_type=MESH)
-
-    for step in range(1, N_SOLID):
-
-        @pl.when(later_s(step))
-        def _():
-            pl.semaphore_signal(barrier, inc=1, device_id={"solid": lax.rem(me_s + step, N_SOLID)}, device_id_type=MESH)
-
-    for step in (1, N_DX - 1):
-        pl.semaphore_signal(barrier, inc=1, device_id={"dx": lax.rem(me_x + step, N_DX)}, device_id_type=MESH)
 
     loads = [
         pltpu.make_async_copy(source, target, in_sem.at[which])
@@ -143,6 +121,32 @@
     for load in loads:
         load.start()
 
+    def rank(place):
+        return jnp.where(place < 4, place, 11 - place)
+
+    def later_s(step):
+        return rank(lax.rem(me_s + step, N_SOLID)) > rank(me_s)
+
+    barrier = pltpu.get_barrier_semaphore()
+    for step in range(1, N_DY):
+
+        @pl.when(me_y + step < N_DY)
+        def _():
+            pl.semaphore_signal(barrier, inc=1, device_id={"dy": me_y + step}, device_id_type=MESH)
+
+    for step in range(1, N_SOLID):
+
+        @pl.when(later_s(step))
+        def _():
+            pl.semaphore_signal(barrier, inc=1, device_id={"solid": lax.rem(me_s + step, N_SOLID)}, device_id_type=MESH)
+
+    up_x, down_x = lax.rem(me_x + 1, N_DX), lax.rem(me_x + N_DX - 1, N_DX)
+    for peer in (up_x, down_x):
+
+        @pl.when(peer > me_x)
+        def _():
+            pl.semaphore_signal(barrier, inc=1, device_id={"dx": peer}, device_id_type=MESH)
+
     def over_solid(source, target, send, recv, own):
         copies = [pltpu.make_async_copy(source.at[:, me_s], target.at[:, me_s], own)]
         for step in range(1, N_SOLID):
@@ -196,6 +200,13 @@
                 for copies in groups:
                     copies[step].start()
 
+    def greet_x():
+        for which, peer in enumerate((up_x, down_x)):
+
+            @pl.when(peer > me_x)
+            def _():
+                pl.semaphore_wait(entered_x.at[which], 1)
+
     def greet_s():
         for step in range(1, N_SOLID):
 
@@ -209,19 +220,27 @@
             copy.wait_recv()
 
     slot_place = iota((1, 1024), 1) & 7
+    slot_device[...] = jnp.where((iota((1024, 128), 0) >> 3) == iota((1024, 128), 1), 1.0, 0.0).astype(BF16)
+    reply_turned[...] = jnp.zeros_like(reply_turned)
     for load in loads[:4]:
         load.wait()
     items[120:128, :] = cells[...].astype(F32)
     rows = jnp.concatenate([items[pl.ds(g, 16, stride=8), :] for g in range(8)], axis=1)
     spread = jnp.concatenate([jnp.where(slot_place == c, rows, 0.0) for c in range(8)], axis=0)
     spread_high, spread_low = split(spread)
-    slot_device = jnp.where((iota((1024, 128), 0) >> 3) == iota((1024, 128), 1), 1.0, 0.0).astype(BF16)
-    packed = dot(spread_high, slot_device) + dot(spread_low, slot_device)
+    packed = dot(spread_high, slot_device[...]) + dot(spread_low, slot_device[...])
     packet[...] = packed.T.reshape(16, 8, 128)
     turned[...] = packed
-    reply_turned[...] = jnp.zeros_like(reply_turned)
-
-    pl.semaphore_wait(barrier, me_y + rank(me_s) + 2)
+
+    earlier_x = jnp.where(me_x > 0, 1, 0) + jnp.where(me_x == N_DX - 1, 1, 0)
+    earlier = me_y + rank(me_s) + earlier_x
+
+    @pl.when(earlier > 0)
+    def _():
+        pl.semaphore_wait(barrier, earlier)
+
+    first = over_dy(packet, middle, send_a, recv_a, own_sem.at[0])
+    start_early(first)
     for step in range(1, N_DY):
 
         @pl.when(me_y >= step)
@@ -239,8 +258,12 @@
                 device_id_type=MESH,
             )
 
-    first = over_dy(packet, middle, send_a, recv_a, own_sem.at[0])
-    start_early(first)
+    for which, peer in enumerate((down_x, up_x)):
+
+        @pl.when(peer < me_x)
+        def _():
+            pl.semaphore_signal(entered_x.at[which], inc=1, device_id={"dx": peer}, device_id_type=MESH)
+
 
     for load in loads[4:]:
         load.wait()
@@ -292,8 +315,6 @@
     reply[...] = reply_turned[...].T.reshape(16, 8, 128)
     second = over_dy(reply, reply_middle, send_c, recv_c, own_sem.at[2])
     start_early(second)
-    start_late([first, second])
-
 
     def remote(source, target, which, where):
         return pltpu.make_async_remote_copy(
@@ -301,7 +322,6 @@
             device_id=where, device_id_type=MESH,
         )
 
-    up_x, down_x = lax.rem(me_x + 1, N_DX), lax.rem(me_x + N_DX - 1, N_DX)
     up_y, down_y = lax.rem(me_y + 1, N_DY), lax.rem(me_y + N_DY - 1, N_DY)
     up_s, down_s = lax.rem(me_s + 1, N_SOLID), lax.rem(me_s + N_SOLID - 1, N_SOLID)
     halo = [
@@ -312,8 +332,6 @@
         remote(edge.at[0], low_z, 4, {"solid": up_s}),
         remote(edge.at[1], high_z, 5, {"solid": down_s}),
     ]
-    start(halo[:4])
-    greet_s()
     edge_row, edge_col = iota((16, 512), 0), iota((16, 512), 1)
     lane_edge = jnp.where(edge_row < 8, 127, 0)
     edge_pick = jnp.where(
@@ -321,7 +339,6 @@
     ).astype(BF16)
     edges = dot_nt(edge_pick, halves[0:192]) + dot_nt(edge_pick, halves[192:384])
     edge[...] = edges.reshape(2, 8, 192)
-    start(halo[4:])
 
     own_visc = visc[...]
     visc_row = jnp.concatenate([own_visc[y : y + 1] for y in range(4)], axis=1)
@@ -337,6 +354,10 @@
         own = field[k].reshape(64, 512)
         applied[k] = (own * (1.0 + ends) + visc_row * dot(stiff, both)).reshape(4, 16, 512)
 
+    start_late([first, second])
+    greet_x()
+    greet_s()
+    start(halo)
     arrive(first)
     third = over_solid(middle, arrived, send_b, recv_b, own_sem.at[1])
     start(third)
@@ -465,6 +486,7 @@
             vmem((8, 64, 64), F32),
             vmem((8, 128), jnp.int32),
             vmem((128, 128), F32),
+            vmem((1024, 128), BF16),
             vmem((3, 4, 16, 512), F32),
             vmem((384, 512), BF16),
             vmem((3, 4, 16, 512), F32),
@@ -490,6 +512,7 @@
             vmem((8, 192), F32),
             dma((8,)),
             dma((4,)),
+            pltpu.SemaphoreType.REGULAR((2,)),
             pltpu.SemaphoreType.REGULAR((N_DY - 1,)),
             pltpu.SemaphoreType.REGULAR((N_SOLID - 1,)),
             dma((N_DY - 1,)),

time: 28.3 us -> 26.9 us (0.951)
  Pallas kernels: 27.5 us -> 26.1 us
    pallas_call x1, Pallas kernels: 26.7 us -> 25.3 us  [shards(): pl.pallas_call(kernel, out_shape=(vmem((768, 128), F32), vmem((72, 128),...]
where the time goes in v4:
time: 26.9 us; the launch traced here: 26.7 us
  Pallas kernels  26.1 us (97%)
  between operations  0.64 us (2%)
    pallas_call x1, Pallas kernels, shards(): pl.pallas_call(kernel, out_shape=(vmem((768, 128), F32), vmem((72, 128),...  25.3 us
    pallas_call x1, Pallas kernels, shards(): pl.pallas_call(place_kernel, out_shape=(jax.ShapeDtypeStruct((768, 128),...  0.77 us

profile of v4, /device:TPU:1, one launch (start us, length us, event | category | flops | bytes accessed | tf_op | source)
XLA Modules:
  0.0 26.7 jit_solution(3516434126853392961)
XLA Ops:
  0.6 25.3 %shard_map.95 = (f32[768,128]{1,0:T(8,128)S(1)}, f32[72,128]{1,0:T(8,128)S(1)}) custom-call(f32[768,128]{1,0:T(8,128)} %bitcast.11, f32[4,128]{1,0:T(4,128)} %bitcast.16, s32[4,128]{1,0:T(4,128)} %bitcast.17, f32[8,64,64]{2,1,0:T(8,128)} %offsets_hbm.1, s32[8,128]{1,0:T(8,128)} %bitcast.15, f32[24,128]{1,0:T(8,128)} %bitcast.13, f32[72,128]{1,0:T(8,128)} %bitcast.12, ...), custom_call_target="tpu_custom_call" | custom-call | tf_op jit(solution)/shard_map/pallas_call | solution.py:477
  26.0 0.8 %shard_map.96 = (f32[768,128]{1,0:T(8,128)}, f32[72,128]{1,0:T(8,128)}) custom-call(f32[768,128]{1,0:T(8,128)S(1)} %get-tuple-element.6.fluid, f32[72,128]{1,0:T(8,128)S(1)} %get-tuple-element.7.deform), custom_call_target="tpu_custom_call" | custom-call | tf_op jit(solution)/shard_map/pallas_call | solution.py:540

commit v5 on v4

--- a/solution.py
+++ b/solution.py
@@ -97,28 +97,24 @@
     vel, visc, config, offsets, cells, items,
     slot_device, field, halves, applied, onehot, shapes, nodal, results, turned, grads,
     packet, middle, arrived, reply, reply_middle, reply_arrived, reply_turned,
-    edge, low_x, high_x, low_y, high_y, low_z, high_z,
-    in_sem, own_sem, entered_x, entered_y, entered_s,
-    send_a, recv_a, send_b, recv_b, send_c, recv_c, send_d, recv_d, send_h, recv_h,
+    edge, sides_x, sides_y, sides_z,
+    in_sem, entered_x, entered_y, entered_s, sends, recvs,
 ):
     me_x, me_y, me_s = lax.axis_index("dx"), lax.axis_index("dy"), lax.axis_index("solid")
 
+    small_loads = [
+        pltpu.make_async_copy(strain_hbm, items.at[0:72], in_sem.at[0]),
+        pltpu.make_async_copy(motion_hbm, items.at[72:96], in_sem.at[0]),
+        pltpu.make_async_copy(coords_hbm, items.at[96:120], in_sem.at[0]),
+    ]
     loads = [
-        pltpu.make_async_copy(source, target, in_sem.at[which])
-        for which, (source, target) in enumerate(
-            (
-                (strain_hbm, items.at[0:72]),
-                (motion_hbm, items.at[72:96]),
-                (coords_hbm, items.at[96:120]),
-                (cells_hbm, cells),
-                (vel_hbm, vel),
-                (offsets_hbm, offsets),
-                (config_hbm, config),
-                (visc_hbm, visc),
-            )
-        )
+        pltpu.make_async_copy(cells_hbm, cells, in_sem.at[1]),
+        pltpu.make_async_copy(vel_hbm, vel, in_sem.at[2]),
+        pltpu.make_async_copy(offsets_hbm, offsets, in_sem.at[3]),
+        pltpu.make_async_copy(config_hbm, config, in_sem.at[4]),
+        pltpu.make_async_copy(visc_hbm, visc, in_sem.at[5]),
     ]
-    for load in loads:
+    for load in small_loads + loads:
         load.start()
 
     def rank(place):
@@ -147,32 +143,32 @@
         def _():
             pl.semaphore_signal(barrier, inc=1, device_id={"dx": peer}, device_id_type=MESH)
 
-    def over_solid(source, target, send, recv, own):
-        copies = [pltpu.make_async_copy(source.at[:, me_s], target.at[:, me_s], own)]
+    def over_solid(source, target, send, recv):
+        copies = [pltpu.make_async_copy(source.at[:, me_s], target.at[:, me_s], recv)]
         for step in range(1, N_SOLID):
             peer = lax.rem(me_s + step, N_SOLID)
             copies.append(
                 pltpu.make_async_remote_copy(
                     src_ref=source.at[:, peer],
                     dst_ref=target.at[:, me_s],
-                    send_sem=send.at[step - 1],
-                    recv_sem=recv.at[step - 1],
+                    send_sem=send,
+                    recv_sem=recv,
                     device_id={"solid": peer},
                     device_id_type=MESH,
                 )
             )
         return copies
 
-    def over_dy(source, target, send, recv, own):
-        copies = [pltpu.make_async_copy(source.at[me_y], target.at[me_y], own)]
+    def over_dy(source, target, send, recv):
+        copies = [pltpu.make_async_copy(source.at[me_y], target.at[me_y], recv)]
         for step in range(1, N_DY):
             peer = lax.rem(me_y + step, N_DY)
             copies.append(
                 pltpu.make_async_remote_copy(
                     src_ref=source.at[peer],
                     dst_ref=target.at[me_y],
-                    send_sem=send.at[step - 1],
-                    recv_sem=recv.at[step - 1],
+                    send_sem=send,
+                    recv_sem=recv,
                     device_id={"dy": peer},
                     device_id_type=MESH,
                 )
@@ -192,38 +188,33 @@
                 copies[step].start()
 
     def start_late(groups):
-        for step in range(1, N_DY):
-
-            @pl.when(me_y + step < N_DY)
+        for batch in range(5):
+            later = jnp.clip(N_DY - 1 - me_y - 3 * batch, 0, 3)
+
+            @pl.when(later > 0)
             def _():
-                pl.semaphore_wait(entered_y.at[step - 1], 1)
-                for copies in groups:
-                    copies[step].start()
-
-    def greet_x():
-        for which, peer in enumerate((up_x, down_x)):
-
-            @pl.when(peer > me_x)
-            def _():
-                pl.semaphore_wait(entered_x.at[which], 1)
-
-    def greet_s():
-        for step in range(1, N_SOLID):
-
-            @pl.when(later_s(step))
-            def _():
-                pl.semaphore_wait(entered_s.at[step - 1], 1)
-
-    def arrive(copies):
-        copies[0].wait()
-        for copy in copies[1:]:
-            copy.wait_recv()
+                pl.semaphore_wait(entered_y.at[batch], later)
+
+            for step in range(3 * batch + 1, 3 * batch + 4):
+
+                @pl.when(me_y + step < N_DY)
+                def _():
+                    for copies in groups:
+                        copies[step].start()
+
+    def greet(entered, later):
+        @pl.when(later > 0)
+        def _():
+            pl.semaphore_wait(entered, later)
+
+    def arrive(source, target, recv):
+        pltpu.make_async_copy(source, target, recv).wait()
 
     slot_place = iota((1, 1024), 1) & 7
     slot_device[...] = jnp.where((iota((1024, 128), 0) >> 3) == iota((1024, 128), 1), 1.0, 0.0).astype(BF16)
     reply_turned[...] = jnp.zeros_like(reply_turned)
-    for load in loads[:4]:
-        load.wait()
+    pltpu.make_async_copy(items.at[0:120], items.at[0:120], in_sem.at[0]).wait()
+    loads[0].wait()
     items[120:128, :] = cells[...].astype(F32)
     rows = jnp.concatenate([items[pl.ds(g, 16, stride=8), :] for g in range(8)], axis=1)
     spread = jnp.concatenate([jnp.where(slot_place == c, rows, 0.0) for c in range(8)], axis=0)
@@ -239,33 +230,33 @@
     def _():
         pl.semaphore_wait(barrier, earlier)
 
-    first = over_dy(packet, middle, send_a, recv_a, own_sem.at[0])
+    first = over_dy(packet, middle, sends.at[0], recvs.at[0])
     start_early(first)
     for step in range(1, N_DY):
 
         @pl.when(me_y >= step)
         def _():
-            pl.semaphore_signal(entered_y.at[step - 1], inc=1, device_id={"dy": me_y - step}, device_id_type=MESH)
+            pl.semaphore_signal(entered_y.at[(step - 1) // 3], inc=1, device_id={"dy": me_y - step}, device_id_type=MESH)
 
     for step in range(1, N_SOLID):
 
         @pl.when(jnp.logical_not(later_s(step)))
         def _():
             pl.semaphore_signal(
-                entered_s.at[N_SOLID - 1 - step],
+                entered_s,
                 inc=1,
                 device_id={"solid": lax.rem(me_s + step, N_SOLID)},
                 device_id_type=MESH,
             )
 
-    for which, peer in enumerate((down_x, up_x)):
+    for peer in (down_x, up_x):
 
         @pl.when(peer < me_x)
         def _():
-            pl.semaphore_signal(entered_x.at[which], inc=1, device_id={"dx": peer}, device_id_type=MESH)
-
-
-    for load in loads[4:]:
+            pl.semaphore_signal(entered_x, inc=1, device_id={"dx": peer}, device_id_type=MESH)
+
+
+    for load in loads[1:]:
         load.wait()
     own_config = config[...]
     config_row = jnp.concatenate([own_config[y : y + 1] for y in range(4)], axis=1)
@@ -313,24 +304,24 @@
         for j in range(3):
             reply_turned[pl.ds(k * 3 + j, 8, stride=16), :] = seen[k * 4 + 1 + j]
     reply[...] = reply_turned[...].T.reshape(16, 8, 128)
-    second = over_dy(reply, reply_middle, send_c, recv_c, own_sem.at[2])
+    second = over_dy(reply, reply_middle, sends.at[1], recvs.at[1])
     start_early(second)
 
     def remote(source, target, which, where):
         return pltpu.make_async_remote_copy(
-            src_ref=source, dst_ref=target, send_sem=send_h.at[which], recv_sem=recv_h.at[which],
+            src_ref=source, dst_ref=target, send_sem=sends.at[which], recv_sem=recvs.at[which],
             device_id=where, device_id_type=MESH,
         )
 
     up_y, down_y = lax.rem(me_y + 1, N_DY), lax.rem(me_y + N_DY - 1, N_DY)
     up_s, down_s = lax.rem(me_s + 1, N_SOLID), lax.rem(me_s + N_SOLID - 1, N_SOLID)
     halo = [
-        remote(field.at[:, 3], low_x, 0, {"dx": up_x}),
-        remote(field.at[:, 0], high_x, 1, {"dx": down_x}),
-        remote(field.at[:, :, 8:16, 384:512], low_y, 2, {"dy": up_y}),
-        remote(field.at[:, :, 0:8, 0:128], high_y, 3, {"dy": down_y}),
-        remote(edge.at[0], low_z, 4, {"solid": up_s}),
-        remote(edge.at[1], high_z, 5, {"solid": down_s}),
+        remote(field.at[:, 3], sides_x.at[0], 4, {"dx": up_x}),
+        remote(field.at[:, 0], sides_x.at[1], 4, {"dx": down_x}),
+        remote(field.at[:, :, 8:16, 384:512], sides_y.at[0], 5, {"dy": up_y}),
+        remote(field.at[:, :, 0:8, 0:128], sides_y.at[1], 5, {"dy": down_y}),
+        remote(edge.at[0], sides_z.at[0], 6, {"solid": up_s}),
+        remote(edge.at[1], sides_z.at[1], 6, {"solid": down_s}),
     ]
     edge_row, edge_col = iota((16, 512), 0), iota((16, 512), 1)
     lane_edge = jnp.where(edge_row < 8, 127, 0)
@@ -355,26 +346,27 @@
         applied[k] = (own * (1.0 + ends) + visc_row * dot(stiff, both)).reshape(4, 16, 512)
 
     start_late([first, second])
-    greet_x()
-    greet_s()
+    greet(entered_x, 2 - earlier_x)
+    greet(entered_s, N_SOLID - 1 - rank(me_s))
     start(halo)
-    arrive(first)
-    third = over_solid(middle, arrived, send_b, recv_b, own_sem.at[1])
+    arrive(packet, middle, recvs.at[0])
+    third = over_solid(middle, arrived, sends.at[2], recvs.at[2])
     start(third)
-    arrive(second)
-    fourth = over_solid(reply_middle, reply_arrived, send_d, recv_d, own_sem.at[3])
+    arrive(reply, reply_middle, recvs.at[1])
+    fourth = over_solid(reply_middle, reply_arrived, sends.at[3], recvs.at[3])
     start(fourth)
 
-    for copy in halo:
-        copy.wait_recv()
+    arrive(sides_x, sides_x, recvs.at[4])
+    arrive(sides_y, sides_y, recvs.at[5])
+    arrive(sides_z, sides_z, recvs.at[6])
     flipped = left_operand(jnp.concatenate([offsets[w].T for w in range(8)], axis=0))
     edge_lane = iota((32, 512), 1)
     edge_line = iota((32, 512), 0)
     edge_place = jnp.where(
         (edge_lane == (edge_line & 7) * 128 + jnp.where((edge_line & 8) == 0, 0, 127)) & ((edge_line & 7) < 4), 1.0, 0.0
     ).astype(BF16)
-    below = jnp.where(me_s > 0, low_z[...], 0.0)
-    above = jnp.where(me_s < N_SOLID - 1, high_z[...], 0.0)
+    below = jnp.where(me_s > 0, sides_z[0], 0.0)
+    above = jnp.where(me_s < N_SOLID - 1, sides_z[1], 0.0)
     edge_high, edge_low = split(jnp.concatenate([below, above], axis=0).T)
     beside = dot(jnp.concatenate([edge_high, edge_low], axis=1), edge_place)
     lane = iota((64, 512), 1) & 127
@@ -391,18 +383,18 @@
         near = jnp.where(place_z == 0, pltpu.roll(previous, 61, 0), 0.0)
         near = near + jnp.where(place_z == 3, pltpu.roll(following, 3, 0), 0.0)
         near = near.reshape(4, 16, 512)
-        lower = jnp.concatenate([jnp.where(me_y > 0, low_y[k], 0.0), own[:, 8:16, :384]], axis=2)
-        upper = jnp.concatenate([own[:, 0:8, 128:], jnp.where(me_y < N_DY - 1, high_y[k], 0.0)], axis=2)
+        lower = jnp.concatenate([jnp.where(me_y > 0, sides_y[0, k], 0.0), own[:, 8:16, :384]], axis=2)
+        upper = jnp.concatenate([own[:, 0:8, 128:], jnp.where(me_y < N_DY - 1, sides_y[1, k], 0.0)], axis=2)
         lower = jnp.where(half_row < 4, pltpu.roll(lower, 4, 1), 0.0)
         upper = jnp.where(half_row >= 4, pltpu.roll(upper, 4, 1), 0.0)
         near = near + jnp.concatenate([lower, upper], axis=1)
-        lower = jnp.where(me_x > 0, low_x[k], 0.0)[None]
-        upper = jnp.where(me_x < N_DX - 1, high_x[k], 0.0)[None]
+        lower = jnp.where(me_x > 0, sides_x[0, k], 0.0)[None]
+        upper = jnp.where(me_x < N_DX - 1, sides_x[1, k], 0.0)[None]
         near = near + jnp.concatenate([lower, jnp.zeros((2, 16, 512), F32), upper], axis=0)
         applied[k] = applied[k] - PENALTY * near
     device_slot = jnp.where((iota((256, 1024), 1) >> 3) == (iota((256, 1024), 0) & 127), 1.0, 0.0).astype(BF16)
 
-    arrive(third)
+    arrive(middle, arrived, recvs.at[2])
     turned[...] = arrived[...].reshape(128, 128).T
     moved = deformed(
         [turned[pl.ds(r, 8, stride=16), :] for r in range(9)],
@@ -436,7 +428,7 @@
         for y in range(4):
             fluid[pl.ds(k * 256 + y, 64, stride=4), :] = result[:, y * 128 : y * 128 + 128]
 
-    arrive(fourth)
+    arrive(reply_middle, reply_arrived, recvs.at[3])
     back_high, back_low = split(reply_arrived[...].reshape(128, 128).T)
     wide = dot(jnp.concatenate([back_high, back_low], axis=1), device_slot)
     slots = jnp.zeros((16, 1024), F32)
@@ -451,11 +443,13 @@
     for k in range(3):
         for l in range(3):
             deform[(k * 3 + l) * 8 : (k * 3 + l) * 8 + 8, :] = moved[k][l]
-    for copies in (first, second, third, fourth):
-        for copy in copies[1:]:
-            copy.wait_send()
-    for copy in halo:
-        copy.wait_send()
+    arrive(packet.at[0:15], middle.at[0:15], sends.at[0])
+    arrive(reply.at[0:15], reply_middle.at[0:15], sends.at[1])
+    arrive(middle.at[0:14], arrived.at[0:14], sends.at[2])
+    arrive(reply_middle.at[0:14], reply_arrived.at[0:14], sends.at[3])
+    arrive(sides_x, sides_x, sends.at[4])
+    arrive(sides_y, sides_y, sends.at[5])
+    arrive(sides_z, sides_z, sends.at[6])
 
 
 def place_kernel(fluid, deform, fluid_hbm, deform_hbm, sem):
@@ -504,27 +498,15 @@
             vmem((16, 8, 128), F32),
             vmem((128, 128), F32),
             vmem((2, 8, 192), F32),
-            vmem((3, 16, 512), F32),
-            vmem((3, 16, 512), F32),
-            vmem((3, 4, 8, 128), F32),
-            vmem((3, 4, 8, 128), F32),
-            vmem((8, 192), F32),
-            vmem((8, 192), F32),
-            dma((8,)),
-            dma((4,)),
-            pltpu.SemaphoreType.REGULAR((2,)),
-            pltpu.SemaphoreType.REGULAR((N_DY - 1,)),
-            pltpu.SemaphoreType.REGULAR((N_SOLID - 1,)),
-            dma((N_DY - 1,)),
-            dma((N_DY - 1,)),
-            dma((N_SOLID - 1,)),
-            dma((N_SOLID - 1,)),
-            dma((N_DY - 1,)),
-            dma((N_DY - 1,)),
-            dma((N_SOLID - 1,)),
-            dma((N_SOLID - 1,)),
+            vmem((2, 3, 16, 512), F32),
+            vmem((2, 3, 4, 8, 128), F32),
+            vmem((2, 8, 192), F32),
             dma((6,)),
-            dma((6,)),
+            pltpu.SemaphoreType.REGULAR,
+            pltpu.SemaphoreType.REGULAR((5,)),
+            pltpu.SemaphoreType.REGULAR,
+            dma((7,)),
+            dma((7,)),
         ],
         compiler_params=pltpu.CompilerParams(collective_id=0, has_side_effects=True),
     )(

time: 26.9 us -> 25.9 us (0.963)
  Pallas kernels: 26.1 us -> 25.1 us
    pallas_call x1, Pallas kernels: 25.3 us -> 24.3 us  [shards(): pl.pallas_call(kernel, out_shape=(vmem((768, 128), F32), vmem((72, 128),...]
where the time goes in v5:
time: 25.9 us; the launch traced here: 25.7 us
  Pallas kernels  25.1 us (97%)
  between operations  0.64 us (2%)
    pallas_call x1, Pallas kernels, shards(): pl.pallas_call(kernel, out_shape=(vmem((768, 128), F32), vmem((72, 128),...  24.3 us
    pallas_call x1, Pallas kernels, shards(): pl.pallas_call(place_kernel, out_shape=(jax.ShapeDtypeStruct((768, 128),...  0.77 us

profile of v5, /device:TPU:1, one launch (start us, length us, event | category | flops | bytes accessed | tf_op | source)
XLA Modules:
  0.0 25.7 jit_solution(8574587254571028773)
XLA Ops:
  0.6 24.3 %shard_map.95 = (f32[768,128]{1,0:T(8,128)S(1)}, f32[72,128]{1,0:T(8,128)S(1)}) custom-call(f32[768,128]{1,0:T(8,128)} %bitcast.11, f32[4,128]{1,0:T(4,128)} %bitcast.16, s32[4,128]{1,0:T(4,128)} %bitcast.17, f32[8,64,64]{2,1,0:T(8,128)} %offsets_hbm.1, s32[8,128]{1,0:T(8,128)} %bitcast.15, f32[24,128]{1,0:T(8,128)} %bitcast.13, f32[72,128]{1,0:T(8,128)} %bitcast.12, ...), custom_call_target="tpu_custom_call" | custom-call | tf_op jit(solution)/shard_map/pallas_call | solution.py:471
  25.0 0.8 %shard_map.96 = (f32[768,128]{1,0:T(8,128)}, f32[72,128]{1,0:T(8,128)}) custom-call(f32[768,128]{1,0:T(8,128)S(1)} %get-tuple-element.6.fluid, f32[72,128]{1,0:T(8,128)S(1)} %get-tuple-element.7.deform), custom_call_target="tpu_custom_call" | custom-call | tf_op jit(solution)/shard_map/pallas_call | solution.py:522

commit v6 on v5

--- a/solution.py
+++ b/solution.py
@@ -238,43 +238,18 @@
         def _():
             pl.semaphore_signal(entered_y.at[(step - 1) // 3], inc=1, device_id={"dy": me_y - step}, device_id_type=MESH)
 
-    for step in range(1, N_SOLID):
-
-        @pl.when(jnp.logical_not(later_s(step)))
-        def _():
-            pl.semaphore_signal(
-                entered_s,
-                inc=1,
-                device_id={"solid": lax.rem(me_s + step, N_SOLID)},
-                device_id_type=MESH,
-            )
-
-    for peer in (down_x, up_x):
-
-        @pl.when(peer < me_x)
-        def _():
-            pl.semaphore_signal(entered_x, inc=1, device_id={"dx": peer}, device_id_type=MESH)
-
-
     for load in loads[1:]:
         load.wait()
     own_config = config[...]
     config_row = jnp.concatenate([own_config[y : y + 1] for y in range(4)], axis=1)
     left = left_operand(offsets[...].reshape(512, 64))
-    for k in range(3):
-        start_field = jnp.concatenate([vel[pl.ds(k * 256 + y, 64, stride=4), :] for y in range(4)], axis=1)
-        own = constrain(start_field, left, config_row)
-        field[k] = own.reshape(4, 16, 512)
-        high, low = split(own)
-        halves[k * 64 : k * 64 + 64] = high
-        halves[192 + k * 64 : 192 + k * 64 + 64] = low
-
     points = [turned[pl.ds(12 + j, 8, stride=16), :] for j in range(3)]
     target = turned[pl.ds(15, 8, stride=16), :]
     polys = [lagrange(point) for point in points]
     cell_index = iota((512, 256), 0).astype(F32)
     node_row = iota((16, 256), 0)
-    for pair in range(4):
+
+    def tables(pair):
         lanes = slice(pair * 256, pair * 256 + 256)
 
         def row(x):
@@ -291,6 +266,17 @@
             shapes[1, at, lanes] = slope_x[a] * plain
             shapes[2, at, lanes] = value_x[a] * along_y
             shapes[3, at, lanes] = value_x[a] * along_z
+
+    for k in range(3):
+        start_field = jnp.concatenate([vel[pl.ds(k * 256 + y, 64, stride=4), :] for y in range(4)], axis=1)
+        own = constrain(start_field, left, config_row)
+        field[k] = own.reshape(4, 16, 512)
+        high, low = split(own)
+        halves[k * 64 : k * 64 + 64] = high
+        halves[192 + k * 64 : 192 + k * 64 + 64] = low
+    for pair in range(4):
+        tables(pair)
+        lanes = slice(pair * 256, pair * 256 + 256)
         gathered = dot(halves[...], onehot[:, lanes])
         for k in range(3):
             nodes = gathered[k * 64 : k * 64 + 64] + gathered[192 + k * 64 : 192 + k * 64 + 64]
@@ -306,6 +292,23 @@
     reply[...] = reply_turned[...].T.reshape(16, 8, 128)
     second = over_dy(reply, reply_middle, sends.at[1], recvs.at[1])
     start_early(second)
+    for step in range(1, N_SOLID):
+
+        @pl.when(jnp.logical_not(later_s(step)))
+        def _():
+            pl.semaphore_signal(
+                entered_s,
+                inc=1,
+                device_id={"solid": lax.rem(me_s + step, N_SOLID)},
+                device_id_type=MESH,
+            )
+
+    for peer in (down_x, up_x):
+
+        @pl.when(peer < me_x)
+        def _():
+            pl.semaphore_signal(entered_x, inc=1, device_id={"dx": peer}, device_id_type=MESH)
+
 
     def remote(source, target, which, where):
         return pltpu.make_async_remote_copy(

time: 25.9 us -> 25.5 us (0.985)
  Pallas kernels: 25.1 us -> 24.7 us
    pallas_call x1, Pallas kernels: 24.3 us -> 23.9 us  [shards(): pl.pallas_call(kernel, out_shape=(vmem((768, 128), F32), vmem((72, 128),...]
where the time goes in v6:
time: 25.5 us; the launch traced here: 25.3 us
  Pallas kernels  24.7 us (97%)
  between operations  0.64 us (3%)
    pallas_call x1, Pallas kernels, shards(): pl.pallas_call(kernel, out_shape=(vmem((768, 128), F32), vmem((72, 128),...  23.9 us
    pallas_call x1, Pallas kernels, shards(): pl.pallas_call(place_kernel, out_shape=(jax.ShapeDtypeStruct((768, 128),...  0.77 us

profile of v6, /device:TPU:1, one launch (start us, length us, event | category | flops | bytes accessed | tf_op | source)
XLA Modules:
  0.0 25.3 jit_solution(5335449346108140114)
XLA Ops:
  0.6 23.9 %shard_map.95 = (f32[768,128]{1,0:T(8,128)S(1)}, f32[72,128]{1,0:T(8,128)S(1)}) custom-call(f32[768,128]{1,0:T(8,128)} %bitcast.11, f32[4,128]{1,0:T(4,128)} %bitcast.16, s32[4,128]{1,0:T(4,128)} %bitcast.17, f32[8,64,64]{2,1,0:T(8,128)} %offsets_hbm.1, s32[8,128]{1,0:T(8,128)} %bitcast.15, f32[24,128]{1,0:T(8,128)} %bitcast.13, f32[72,128]{1,0:T(8,128)} %bitcast.12, ...), custom_call_target="tpu_custom_call" | custom-call | tf_op jit(solution)/shard_map/pallas_call | solution.py:474
  24.6 0.8 %shard_map.96 = (f32[768,128]{1,0:T(8,128)}, f32[72,128]{1,0:T(8,128)}) custom-call(f32[768,128]{1,0:T(8,128)S(1)} %get-tuple-element.6.fluid, f32[72,128]{1,0:T(8,128)S(1)} %get-tuple-element.7.deform), custom_call_target="tpu_custom_call" | custom-call | tf_op jit(solution)/shard_map/pallas_call | solution.py:525

commit v7 on v6

--- a/solution.py
+++ b/solution.py
@@ -232,12 +232,6 @@
 
     first = over_dy(packet, middle, sends.at[0], recvs.at[0])
     start_early(first)
-    for step in range(1, N_DY):
-
-        @pl.when(me_y >= step)
-        def _():
-            pl.semaphore_signal(entered_y.at[(step - 1) // 3], inc=1, device_id={"dy": me_y - step}, device_id_type=MESH)
-
     for load in loads[1:]:
         load.wait()
     own_config = config[...]
@@ -292,6 +286,12 @@
     reply[...] = reply_turned[...].T.reshape(16, 8, 128)
     second = over_dy(reply, reply_middle, sends.at[1], recvs.at[1])
     start_early(second)
+    for step in range(1, N_DY):
+
+        @pl.when(me_y >= step)
+        def _():
+            pl.semaphore_signal(entered_y.at[(step - 1) // 3], inc=1, device_id={"dy": me_y - step}, device_id_type=MESH)
+
     for step in range(1, N_SOLID):
 
         @pl.when(jnp.logical_not(later_s(step)))

time: 25.5 us -> 24.9 us (0.976)
  Pallas kernels: 24.7 us -> 24.1 us
    pallas_call x1, Pallas kernels: 23.9 us -> 23.3 us  [shards(): pl.pallas_call(kernel, out_shape=(vmem((768, 128), F32), vmem((72, 128),...]
where the time goes in v7:
time: 24.9 us; the launch traced here: 24.7 us
  Pallas kernels  24.1 us (97%)
  between operations  0.64 us (3%)
    pallas_call x1, Pallas kernels, shards(): pl.pallas_call(kernel, out_shape=(vmem((768, 128), F32), vmem((72, 128),...  23.3 us
    pallas_call x1, Pallas kernels, shards(): pl.pallas_call(place_kernel, out_shape=(jax.ShapeDtypeStruct((768, 128),...  0.77 us

profile of v7, /device:TPU:1, one launch (start us, length us, event | category | flops | bytes accessed | tf_op | source)
XLA Modules:
  0.0 24.7 jit_solution(4185732619230717996)
XLA Ops:
  0.6 23.3 %shard_map.95 = (f32[768,128]{1,0:T(8,128)S(1)}, f32[72,128]{1,0:T(8,128)S(1)}) custom-call(f32[768,128]{1,0:T(8,128)} %bitcast.11, f32[4,128]{1,0:T(4,128)} %bitcast.16, s32[4,128]{1,0:T(4,128)} %bitcast.17, f32[8,64,64]{2,1,0:T(8,128)} %offsets_hbm.1, s32[8,128]{1,0:T(8,128)} %bitcast.15, f32[24,128]{1,0:T(8,128)} %bitcast.13, f32[72,128]{1,0:T(8,128)} %bitcast.12, ...), custom_call_target="tpu_custom_call" | custom-call | tf_op jit(solution)/shard_map/pallas_call | solution.py:474
  24.0 0.8 %shard_map.96 = (f32[768,128]{1,0:T(8,128)}, f32[72,128]{1,0:T(8,128)}) custom-call(f32[768,128]{1,0:T(8,128)S(1)} %get-tuple-element.6.fluid, f32[72,128]{1,0:T(8,128)S(1)} %get-tuple-element.7.deform), custom_call_target="tpu_custom_call" | custom-call | tf_op jit(solution)/shard_map/pallas_call | solution.py:525
